TPU v7x, 1024 devices: a whole 8x8x8 slice. The times are simulated.
1024 devices in a mesh: phase: 8 (over x), blk: 32 (over z_hi, y), head: 4 (over z_lo, core).
Axes of the slice: x: 8, y: 8, z: 8 (z_hi: 4, z_lo: 2; z = z_hi * 2 + z_lo), core: 2. Of those that a mesh axis runs over, the one named last changes fastest.
Arguments:
- visual: bfloat16 [131072, 4096], P(('phase', 'blk')), may hold values from -8 to 8
- key_weight: bfloat16 [4096, 1024], P(None, 'head'), may hold values from -1 to 1
- value_weight: bfloat16 [4096, 1024], P(None, 'head'), may hold values from -0.09375 to 0.09375
- queries: bfloat16 [512, 4096], P('blk', 'head'), may hold values from -512 to 512
- bounds: int32 [512, 2], P('blk'), may hold values from 0 to 131072, as said below
- tile_mask: int32 [32, 256], replicated, may hold values from 0 to 1
Outputs:
- attended: bfloat16 [512, 4096], P('blk', 'head')
Inputs may be any that keep to these rules, and one draw needn't show every extreme that they name: For each text row 0 <= bounds[i, 0] < bounds[i, 1] <= 131072; the first row starts at 0 and the last ends at 131072; every text row may see all 512 rows of at least one visual tile.
All inputs are finite; a program needn't handle non-finite values.
Results may differ from a plain program's by a relative error of at most 0.015.
Values may be sent and summed in bfloat16 or wider, within the bound.
No kernel may reach another device: no remote copies, remote signals or barrier semaphores. Data moves between devices by JAX's collectives and lax.ppermute only.
A program may use at most 32 MiB of HBM per device.

v0:
```python
import math

import jax
import jax.numpy as jnp
from jax import lax
from jax.sharding import PartitionSpec as P

HD = 128


def shifted(block, axis, distance):
    devices = range(lax.axis_size(axis))
    route = [((i - distance) % len(devices), i) for i in devices]
    return lax.ppermute(block, axis, route)


def merged(value, axis, join):
    pieces = jax.tree.map(lambda part: lax.all_gather(part, axis), value)
    head = jax.tree.map(lambda part: part[0], pieces)
    tail = jax.tree.map(lambda part: part[1:], pieces)
    running, _ = lax.scan(lambda running, piece: (join(running, piece), None), head, tail)
    return running


def combine(first, second):
    top_first, total_first, summed_first = first
    top_second, total_second, summed_second = second
    row_top = jnp.maximum(top_first, top_second)
    factor_first = jnp.exp(top_first - row_top)
    factor_second = jnp.exp(top_second - row_top)
    row_total = total_first * factor_first + total_second * factor_second
    summed = summed_first * factor_first[..., None] + summed_second * factor_second[..., None]
    return (row_top, row_total, summed)


def attend(state, query_block, key_block, value_block, permitted):
    scale = 1.0 / math.sqrt(HD)
    old_top, old_total, old_summed = state
    scores = (
        jnp.einsum("tkgd,vkd->tkgv", query_block, key_block, preferred_element_type=jnp.float32)
        * scale
    )
    visible = permitted[:, None, None, :]
    masked = jnp.where(visible, scores, -1e30)
    row_top = jnp.maximum(old_top, jnp.max(masked, axis=3))
    factor = jnp.exp(old_top - row_top)
    weights = jnp.where(visible, jnp.exp(masked - row_top[..., None]), 0.0)
    row_total = old_total * factor + jnp.sum(weights, axis=3)
    summed = old_summed * factor[..., None] + jnp.einsum(
        "tkgv,vkd->tkgd",
        weights.astype(jnp.bfloat16),
        value_block,
        preferred_element_type=jnp.float32,
    )
    return (row_top, row_total, summed)


def per_device(visual, key_weight, value_weight, queries, bounds, tile_mask):
    vis_rows = visual.shape[0]
    text_rows = queries.shape[0]
    kv_heads = key_weight.shape[1] // HD
    group = queries.shape[1] // HD // kv_heads
    keys = jnp.dot(visual, key_weight, preferred_element_type=jnp.float32).astype(jnp.bfloat16)
    values = jnp.dot(visual, value_weight, preferred_element_type=jnp.float32).astype(jnp.bfloat16)
    keys = keys.reshape(vis_rows, kv_heads, HD)
    values = values.reshape(vis_rows, kv_heads, HD)
    query_block = queries.reshape(text_rows, kv_heads, group, HD)
    blocks = lax.axis_size("blk")
    blk_index = lax.axis_index("blk")
    phase_index = lax.axis_index("phase")
    my_tile = phase_index * blocks + blk_index
    vis_start = my_tile * vis_rows
    vis_columns = vis_start + jnp.arange(vis_rows, dtype=jnp.int32)

    def cycle_turn(turn_index, carry):
        moving_query, moving_bounds, row_top, row_total, summed = carry
        tile = (blk_index - turn_index) % blocks
        tile_bit = lax.dynamic_slice(tile_mask, (tile, my_tile), (1, 1))[0, 0]
        lower = moving_bounds[:, 0].astype(jnp.int32)
        upper = moving_bounds[:, 1].astype(jnp.int32)
        permitted = (
            (vis_columns[None, :] >= lower[:, None])
            & (vis_columns[None, :] < upper[:, None])
            & (tile_bit == 1)
        )
        row_top, row_total, summed = attend(
            (row_top, row_total, summed), moving_query, keys, values, permitted
        )
        moving_query = shifted(moving_query, "blk", 1)
        moving_bounds, row_top, row_total, summed = shifted(
            (moving_bounds, row_top, row_total, summed), "blk", 1
        )
        return (moving_query, moving_bounds, row_top, row_total, summed)

    start_top = jnp.full((text_rows, kv_heads, group), -1e30, jnp.float32)
    start_total = jnp.zeros((text_rows, kv_heads, group), jnp.float32)
    start_summed = jnp.zeros((text_rows, kv_heads, group, HD), jnp.float32)
    carry = (query_block, bounds.astype(jnp.float32), start_top, start_total, start_summed)
    carry = lax.fori_loop(0, blocks, cycle_turn, carry)
    state = (carry[2], carry[3], carry[4])
    row_top, row_total, summed = merged(state, "phase", combine)
    result = summed / row_total[..., None]
    return result.reshape(text_rows, kv_heads * group * HD).astype(jnp.bfloat16)


def solution(mesh):
    return jax.shard_map(
        per_device,
        mesh=mesh,
        in_specs=(
            P(("phase", "blk"), None),
            P(None, "head"),
            P(None, "head"),
            P("blk", "head"),
            P("blk", None),
            P(),
        ),
        out_specs=P("blk", "head"),
        check_vma=False,
    )
```

profile of v0, /device:TPU:8, one launch (start us, length us, event | category | flops | bytes accessed | tf_op | source)
XLA Modules:
  0.0 861.2 jit_solution(15847940698302411987)
XLA Ops:
  9.8 772.0 %while.39 = (s32[]{:T(128)}, bf16[16,2,4,128]{3,0,2,1:T(8,128)(2,1)S(1)}, f32[16,2]{0,1:T(2,128)S(1)}, f32[16,2,4]{0,2,1:T(4,128)S(1)}, f32[16,2,4]{0,2,1:T(4,12...) while((s32[]{:T(128)}, ...), condition=%wide.region_3.4_spmd.clone, body=%wide.region_0.3_spmd.clone.sunk | while | flops 34210608 | bytes 1983130 | solution.py:99
  31.0 7.2 collective-permute-done.2
  81.3 7.7 collective-permute-done.1
  106.6 7.7 collective-permute-done.1
  121.1 6.4 collective-permute-start.2
  127.5 5.4 collective-permute-start.3
  134.9 7.7 collective-permute-done.1
  159.1 5.7 collective-permute-done.1
  184.1 7.7 collective-permute-done.1
  271.2 7.7 collective-permute-done.1
  296.4 7.7 collective-permute-done.1
  311.0 6.4 collective-permute-start.2
  324.7 7.8 collective-permute-done.1
  348.9 5.7 collective-permute-done.1
  374.0 7.8 collective-permute-done.1
  461.0 7.7 collective-permute-done.1
  486.3 7.7 collective-permute-done.1
  500.8 6.4 collective-permute-start.2
  514.5 7.7 collective-permute-done.1
  538.8 5.7 collective-permute-done.1
  556.5 5.4 collective-permute-start.3
  563.9 7.7 collective-permute-done.1
  650.8 7.8 collective-permute-done.1
  668.9 5.4 collective-permute-start.3
  676.2 7.7 collective-permute-done.1
  690.8 6.7 collective-permute-start.2
  697.5 5.4 collective-permute-start.3
  704.8 7.7 collective-permute-done.1
  753.7 7.7 collective-permute-done.1
  781.8 25.2 %all-gather.2 = f32[128,2,4,128]{3,0,2,1:T(8,128)S(1)} all-gather(f32[16,2,4,128]{3,0,2,1:T(8,128)S(1)} %get-tuple-element.338), channel_id=4, replica_groups=mesh['phase'=8,'blk'=32,'head'=4] {'phase'}, dimensions={0}, use_global_device_ids=true | all-gather | bytes 589824 | tf_op jit(solution)/shard_map/all_gather | solution.py:18
  807.2 24.6 %all-gather = f32[128,2,4]{2,1,0:T(2,128)S(1)} all-gather(f32[16,2,4]{2,1,0:T(2,128)S(1)} %copy.31), channel_id=2, replica_groups=mesh['phase'=8,'blk'=32,'head'=4] {'phase'}, dimensions={0}, use_global_device_ids=true | all-gather | bytes 4608 | tf_op jit(solution)/shard_map/all_gather | solution.py:18
  832.0 24.6 %all-gather.1 = f32[128,2,4]{2,1,0:T(2,128)S(1)} all-gather(f32[16,2,4]{2,1,0:T(2,128)S(1)} %copy.32), channel_id=3, replica_groups=mesh['phase'=8,'blk'=32,'head'=4] {'phase'}, dimensions={0}, use_global_device_ids=true | all-gather | bytes 4608 | tf_op jit(solution)/shard_map/all_gather | solution.py:18
  (712 shorter events, 569.1 us)
Async XLA Ops:
  12.7 29.4 %collective-permute-start.4 = (f32[16,2,4,128]{3,0,2,1:T(8,128)S(1)}, f32[16,2,4,128]{3,0,2,1:T(8,128)S(1)}, u32[]{:S(2)}, u32[]{:S(2)}) collective-permute-start(f32[16,2,4,128]{3,0,2,1:T(8,128)S(1)} %fusion.40), channel_id=1, source_target_pairs={{124,0},{0,4},{4,8},{8,12},{12,16},{16,20},{20,24},{24,28},{28,32}... | collective-permute-start | bytes 196616 | tf_op jit(solution)/shard_map/while/body/eval_jaxpr/ppermute | solution.py:14
  16.3 25.8 %collective-permute-start = (bf16[16,2,4,128]{3,0,2,1:T(8,128)(2,1)S(1)}, bf16[16,2,4,128]{3,0,2,1:T(8,128)(2,1)S(1)}, u32[]{:S(2)}, u32[]{:S(2)}) collective-permute-start(bf16[16,2,4,128]{3,0,2,1:T(8,128)(2,1)S(1)} %copy.67), channel_id=1, source_target_pairs={{124,0},{0,4},{4,8},{8,12},{12,16},{16,20},{20,24},{24,28},{28,32}... | collective-permute-start | bytes 98312 | tf_op jit(solution)/shard_map/while/body/eval_jaxpr/ppermute | solution.py:14
  65.3 23.8 %collective-permute-start.4 = (f32[16,2,4,128]{3,0,2,1:T(8,128)S(1)}, f32[16,2,4,128]{3,0,2,1:T(8,128)S(1)}, u32[]{:S(2)}, u32[]{:S(2)}) collective-permute-start(f32[16,2,4,128]{3,0,2,1:T(8,128)S(1)} %fusion.40), channel_id=1, source_target_pairs={{124,0},{0,4},{4,8},{8,12},{12,16},{16,20},{20,24},{24,28},{28,32}... | collective-permute-start | bytes 196616 | tf_op jit(solution)/shard_map/while/body/eval_jaxpr/ppermute | solution.py:14
  67.2 21.9 %collective-permute-start = (bf16[16,2,4,128]{3,0,2,1:T(8,128)(2,1)S(1)}, bf16[16,2,4,128]{3,0,2,1:T(8,128)(2,1)S(1)}, u32[]{:S(2)}, u32[]{:S(2)}) collective-permute-start(bf16[16,2,4,128]{3,0,2,1:T(8,128)(2,1)S(1)} %copy.67), channel_id=1, source_target_pairs={{124,0},{0,4},{4,8},{8,12},{12,16},{16,20},{20,24},{24,28},{28,32}... | collective-permute-start | bytes 98312 | tf_op jit(solution)/shard_map/while/body/eval_jaxpr/ppermute | solution.py:14
  92.0 22.3 %collective-permute-start.4 = (f32[16,2,4,128]{3,0,2,1:T(8,128)S(1)}, f32[16,2,4,128]{3,0,2,1:T(8,128)S(1)}, u32[]{:S(2)}, u32[]{:S(2)}) collective-permute-start(f32[16,2,4,128]{3,0,2,1:T(8,128)S(1)} %fusion.40), channel_id=1, source_target_pairs={{124,0},{0,4},{4,8},{8,12},{12,16},{16,20},{20,24},{24,28},{28,32}... | collective-permute-start | bytes 196616 | tf_op jit(solution)/shard_map/while/body/eval_jaxpr/ppermute | solution.py:14
  117.3 25.3 %collective-permute-start.4 = (f32[16,2,4,128]{3,0,2,1:T(8,128)S(1)}, f32[16,2,4,128]{3,0,2,1:T(8,128)S(1)}, u32[]{:S(2)}, u32[]{:S(2)}) collective-permute-start(f32[16,2,4,128]{3,0,2,1:T(8,128)S(1)} %fusion.40), channel_id=1, source_target_pairs={{124,0},{0,4},{4,8},{8,12},{12,16},{16,20},{20,24},{24,28},{28,32}... | collective-permute-start | bytes 196616 | tf_op jit(solution)/shard_map/while/body/eval_jaxpr/ppermute | solution.py:14
  119.2 23.4 %collective-permute-start = (bf16[16,2,4,128]{3,0,2,1:T(8,128)(2,1)S(1)}, bf16[16,2,4,128]{3,0,2,1:T(8,128)(2,1)S(1)}, u32[]{:S(2)}, u32[]{:S(2)}) collective-permute-start(bf16[16,2,4,128]{3,0,2,1:T(8,128)(2,1)S(1)} %copy.67), channel_id=1, source_target_pairs={{124,0},{0,4},{4,8},{8,12},{12,16},{16,20},{20,24},{24,28},{28,32}... | collective-permute-start | bytes 98312 | tf_op jit(solution)/shard_map/while/body/eval_jaxpr/ppermute | solution.py:14
  167.8 24.1 %collective-permute-start.4 = (f32[16,2,4,128]{3,0,2,1:T(8,128)S(1)}, f32[16,2,4,128]{3,0,2,1:T(8,128)S(1)}, u32[]{:S(2)}, u32[]{:S(2)}) collective-permute-start(f32[16,2,4,128]{3,0,2,1:T(8,128)S(1)} %fusion.40), channel_id=1, source_target_pairs={{124,0},{0,4},{4,8},{8,12},{12,16},{16,20},{20,24},{24,28},{28,32}... | collective-permute-start | bytes 196616 | tf_op jit(solution)/shard_map/while/body/eval_jaxpr/ppermute | solution.py:14
  169.7 22.2 %collective-permute-start = (bf16[16,2,4,128]{3,0,2,1:T(8,128)(2,1)S(1)}, bf16[16,2,4,128]{3,0,2,1:T(8,128)(2,1)S(1)}, u32[]{:S(2)}, u32[]{:S(2)}) collective-permute-start(bf16[16,2,4,128]{3,0,2,1:T(8,128)(2,1)S(1)} %copy.67), channel_id=1, source_target_pairs={{124,0},{0,4},{4,8},{8,12},{12,16},{16,20},{20,24},{24,28},{28,32}... | collective-permute-start | bytes 98312 | tf_op jit(solution)/shard_map/while/body/eval_jaxpr/ppermute | solution.py:14
  255.8 23.1 %collective-permute-start.4 = (f32[16,2,4,128]{3,0,2,1:T(8,128)S(1)}, f32[16,2,4,128]{3,0,2,1:T(8,128)S(1)}, u32[]{:S(2)}, u32[]{:S(2)}) collective-permute-start(f32[16,2,4,128]{3,0,2,1:T(8,128)S(1)} %fusion.40), channel_id=1, source_target_pairs={{124,0},{0,4},{4,8},{8,12},{12,16},{16,20},{20,24},{24,28},{28,32}... | collective-permute-start | bytes 196616 | tf_op jit(solution)/shard_map/while/body/eval_jaxpr/ppermute | solution.py:14
  257.7 21.2 %collective-permute-start = (bf16[16,2,4,128]{3,0,2,1:T(8,128)(2,1)S(1)}, bf16[16,2,4,128]{3,0,2,1:T(8,128)(2,1)S(1)}, u32[]{:S(2)}, u32[]{:S(2)}) collective-permute-start(bf16[16,2,4,128]{3,0,2,1:T(8,128)(2,1)S(1)} %copy.67), channel_id=1, source_target_pairs={{124,0},{0,4},{4,8},{8,12},{12,16},{16,20},{20,24},{24,28},{28,32}... | collective-permute-start | bytes 98312 | tf_op jit(solution)/shard_map/while/body/eval_jaxpr/ppermute | solution.py:14
  281.8 22.4 %collective-permute-start.4 = (f32[16,2,4,128]{3,0,2,1:T(8,128)S(1)}, f32[16,2,4,128]{3,0,2,1:T(8,128)S(1)}, u32[]{:S(2)}, u32[]{:S(2)}) collective-permute-start(f32[16,2,4,128]{3,0,2,1:T(8,128)S(1)} %fusion.40), channel_id=1, source_target_pairs={{124,0},{0,4},{4,8},{8,12},{12,16},{16,20},{20,24},{24,28},{28,32}... | collective-permute-start | bytes 196616 | tf_op jit(solution)/shard_map/while/body/eval_jaxpr/ppermute | solution.py:14
  307.1 25.3 %collective-permute-start.4 = (f32[16,2,4,128]{3,0,2,1:T(8,128)S(1)}, f32[16,2,4,128]{3,0,2,1:T(8,128)S(1)}, u32[]{:S(2)}, u32[]{:S(2)}) collective-permute-start(f32[16,2,4,128]{3,0,2,1:T(8,128)S(1)} %fusion.40), channel_id=1, source_target_pairs={{124,0},{0,4},{4,8},{8,12},{12,16},{16,20},{20,24},{24,28},{28,32}... | collective-permute-start | bytes 196616 | tf_op jit(solution)/shard_map/while/body/eval_jaxpr/ppermute | solution.py:14
  309.0 23.4 %collective-permute-start = (bf16[16,2,4,128]{3,0,2,1:T(8,128)(2,1)S(1)}, bf16[16,2,4,128]{3,0,2,1:T(8,128)(2,1)S(1)}, u32[]{:S(2)}, u32[]{:S(2)}) collective-permute-start(bf16[16,2,4,128]{3,0,2,1:T(8,128)(2,1)S(1)} %copy.67), channel_id=1, source_target_pairs={{124,0},{0,4},{4,8},{8,12},{12,16},{16,20},{20,24},{24,28},{28,32}... | collective-permute-start | bytes 98312 | tf_op jit(solution)/shard_map/while/body/eval_jaxpr/ppermute | solution.py:14
  357.6 24.2 %collective-permute-start.4 = (f32[16,2,4,128]{3,0,2,1:T(8,128)S(1)}, f32[16,2,4,128]{3,0,2,1:T(8,128)S(1)}, u32[]{:S(2)}, u32[]{:S(2)}) collective-permute-start(f32[16,2,4,128]{3,0,2,1:T(8,128)S(1)} %fusion.40), channel_id=1, source_target_pairs={{124,0},{0,4},{4,8},{8,12},{12,16},{16,20},{20,24},{24,28},{28,32}... | collective-permute-start | bytes 196616 | tf_op jit(solution)/shard_map/while/body/eval_jaxpr/ppermute | solution.py:14
  359.5 22.3 %collective-permute-start = (bf16[16,2,4,128]{3,0,2,1:T(8,128)(2,1)S(1)}, bf16[16,2,4,128]{3,0,2,1:T(8,128)(2,1)S(1)}, u32[]{:S(2)}, u32[]{:S(2)}) collective-permute-start(bf16[16,2,4,128]{3,0,2,1:T(8,128)(2,1)S(1)} %copy.67), channel_id=1, source_target_pairs={{124,0},{0,4},{4,8},{8,12},{12,16},{16,20},{20,24},{24,28},{28,32}... | collective-permute-start | bytes 98312 | tf_op jit(solution)/shard_map/while/body/eval_jaxpr/ppermute | solution.py:14
  445.7 23.1 %collective-permute-start.4 = (f32[16,2,4,128]{3,0,2,1:T(8,128)S(1)}, f32[16,2,4,128]{3,0,2,1:T(8,128)S(1)}, u32[]{:S(2)}, u32[]{:S(2)}) collective-permute-start(f32[16,2,4,128]{3,0,2,1:T(8,128)S(1)} %fusion.40), channel_id=1, source_target_pairs={{124,0},{0,4},{4,8},{8,12},{12,16},{16,20},{20,24},{24,28},{28,32}... | collective-permute-start | bytes 196616 | tf_op jit(solution)/shard_map/while/body/eval_jaxpr/ppermute | solution.py:14
  447.6 21.1 %collective-permute-start = (bf16[16,2,4,128]{3,0,2,1:T(8,128)(2,1)S(1)}, bf16[16,2,4,128]{3,0,2,1:T(8,128)(2,1)S(1)}, u32[]{:S(2)}, u32[]{:S(2)}) collective-permute-start(bf16[16,2,4,128]{3,0,2,1:T(8,128)(2,1)S(1)} %copy.67), channel_id=1, source_target_pairs={{124,0},{0,4},{4,8},{8,12},{12,16},{16,20},{20,24},{24,28},{28,32}... | collective-permute-start | bytes 98312 | tf_op jit(solution)/shard_map/while/body/eval_jaxpr/ppermute | solution.py:14
  471.7 22.4 %collective-permute-start.4 = (f32[16,2,4,128]{3,0,2,1:T(8,128)S(1)}, f32[16,2,4,128]{3,0,2,1:T(8,128)S(1)}, u32[]{:S(2)}, u32[]{:S(2)}) collective-permute-start(f32[16,2,4,128]{3,0,2,1:T(8,128)S(1)} %fusion.40), channel_id=1, source_target_pairs={{124,0},{0,4},{4,8},{8,12},{12,16},{16,20},{20,24},{24,28},{28,32}... | collective-permute-start | bytes 196616 | tf_op jit(solution)/shard_map/while/body/eval_jaxpr/ppermute | solution.py:14
  473.6 20.4 %collective-permute-start = (bf16[16,2,4,128]{3,0,2,1:T(8,128)(2,1)S(1)}, bf16[16,2,4,128]{3,0,2,1:T(8,128)(2,1)S(1)}, u32[]{:S(2)}, u32[]{:S(2)}) collective-permute-start(bf16[16,2,4,128]{3,0,2,1:T(8,128)(2,1)S(1)} %copy.67), channel_id=1, source_target_pairs={{124,0},{0,4},{4,8},{8,12},{12,16},{16,20},{20,24},{24,28},{28,32}... | collective-permute-start | bytes 98312 | tf_op jit(solution)/shard_map/while/body/eval_jaxpr/ppermute | solution.py:14
  496.9 25.3 %collective-permute-start.4 = (f32[16,2,4,128]{3,0,2,1:T(8,128)S(1)}, f32[16,2,4,128]{3,0,2,1:T(8,128)S(1)}, u32[]{:S(2)}, u32[]{:S(2)}) collective-permute-start(f32[16,2,4,128]{3,0,2,1:T(8,128)S(1)} %fusion.40), channel_id=1, source_target_pairs={{124,0},{0,4},{4,8},{8,12},{12,16},{16,20},{20,24},{24,28},{28,32}... | collective-permute-start | bytes 196616 | tf_op jit(solution)/shard_map/while/body/eval_jaxpr/ppermute | solution.py:14
  498.9 23.4 %collective-permute-start = (bf16[16,2,4,128]{3,0,2,1:T(8,128)(2,1)S(1)}, bf16[16,2,4,128]{3,0,2,1:T(8,128)(2,1)S(1)}, u32[]{:S(2)}, u32[]{:S(2)}) collective-permute-start(bf16[16,2,4,128]{3,0,2,1:T(8,128)(2,1)S(1)} %copy.67), channel_id=1, source_target_pairs={{124,0},{0,4},{4,8},{8,12},{12,16},{16,20},{20,24},{24,28},{28,32}... | collective-permute-start | bytes 98312 | tf_op jit(solution)/shard_map/while/body/eval_jaxpr/ppermute | solution.py:14
  547.4 24.2 %collective-permute-start.4 = (f32[16,2,4,128]{3,0,2,1:T(8,128)S(1)}, f32[16,2,4,128]{3,0,2,1:T(8,128)S(1)}, u32[]{:S(2)}, u32[]{:S(2)}) collective-permute-start(f32[16,2,4,128]{3,0,2,1:T(8,128)S(1)} %fusion.40), channel_id=1, source_target_pairs={{124,0},{0,4},{4,8},{8,12},{12,16},{16,20},{20,24},{24,28},{28,32}... | collective-permute-start | bytes 196616 | tf_op jit(solution)/shard_map/while/body/eval_jaxpr/ppermute | solution.py:14
  549.4 22.3 %collective-permute-start = (bf16[16,2,4,128]{3,0,2,1:T(8,128)(2,1)S(1)}, bf16[16,2,4,128]{3,0,2,1:T(8,128)(2,1)S(1)}, u32[]{:S(2)}, u32[]{:S(2)}) collective-permute-start(bf16[16,2,4,128]{3,0,2,1:T(8,128)(2,1)S(1)} %copy.67), channel_id=1, source_target_pairs={{124,0},{0,4},{4,8},{8,12},{12,16},{16,20},{20,24},{24,28},{28,32}... | collective-permute-start | bytes 98312 | tf_op jit(solution)/shard_map/while/body/eval_jaxpr/ppermute | solution.py:14
  635.5 23.0 %collective-permute-start.4 = (f32[16,2,4,128]{3,0,2,1:T(8,128)S(1)}, f32[16,2,4,128]{3,0,2,1:T(8,128)S(1)}, u32[]{:S(2)}, u32[]{:S(2)}) collective-permute-start(f32[16,2,4,128]{3,0,2,1:T(8,128)S(1)} %fusion.40), channel_id=1, source_target_pairs={{124,0},{0,4},{4,8},{8,12},{12,16},{16,20},{20,24},{24,28},{28,32}... | collective-permute-start | bytes 196616 | tf_op jit(solution)/shard_map/while/body/eval_jaxpr/ppermute | solution.py:14
  637.5 21.1 %collective-permute-start = (bf16[16,2,4,128]{3,0,2,1:T(8,128)(2,1)S(1)}, bf16[16,2,4,128]{3,0,2,1:T(8,128)(2,1)S(1)}, u32[]{:S(2)}, u32[]{:S(2)}) collective-permute-start(bf16[16,2,4,128]{3,0,2,1:T(8,128)(2,1)S(1)} %copy.67), channel_id=1, source_target_pairs={{124,0},{0,4},{4,8},{8,12},{12,16},{16,20},{20,24},{24,28},{28,32}... | collective-permute-start | bytes 98312 | tf_op jit(solution)/shard_map/while/body/eval_jaxpr/ppermute | solution.py:14
  661.5 22.5 %collective-permute-start.4 = (f32[16,2,4,128]{3,0,2,1:T(8,128)S(1)}, f32[16,2,4,128]{3,0,2,1:T(8,128)S(1)}, u32[]{:S(2)}, u32[]{:S(2)}) collective-permute-start(f32[16,2,4,128]{3,0,2,1:T(8,128)S(1)} %fusion.40), channel_id=1, source_target_pairs={{124,0},{0,4},{4,8},{8,12},{12,16},{16,20},{20,24},{24,28},{28,32}... | collective-permute-start | bytes 196616 | tf_op jit(solution)/shard_map/while/body/eval_jaxpr/ppermute | solution.py:14
  663.4 20.6 %collective-permute-start = (bf16[16,2,4,128]{3,0,2,1:T(8,128)(2,1)S(1)}, bf16[16,2,4,128]{3,0,2,1:T(8,128)(2,1)S(1)}, u32[]{:S(2)}, u32[]{:S(2)}) collective-permute-start(bf16[16,2,4,128]{3,0,2,1:T(8,128)(2,1)S(1)} %copy.67), channel_id=1, source_target_pairs={{124,0},{0,4},{4,8},{8,12},{12,16},{16,20},{20,24},{24,28},{28,32}... | collective-permute-start | bytes 98312 | tf_op jit(solution)/shard_map/while/body/eval_jaxpr/ppermute | solution.py:14
  686.9 25.7 %collective-permute-start.4 = (f32[16,2,4,128]{3,0,2,1:T(8,128)S(1)}, f32[16,2,4,128]{3,0,2,1:T(8,128)S(1)}, u32[]{:S(2)}, u32[]{:S(2)}) collective-permute-start(f32[16,2,4,128]{3,0,2,1:T(8,128)S(1)} %fusion.40), channel_id=1, source_target_pairs={{124,0},{0,4},{4,8},{8,12},{12,16},{16,20},{20,24},{24,28},{28,32}... | collective-permute-start | bytes 196616 | tf_op jit(solution)/shard_map/while/body/eval_jaxpr/ppermute | solution.py:14
  688.8 23.7 %collective-permute-start = (bf16[16,2,4,128]{3,0,2,1:T(8,128)(2,1)S(1)}, bf16[16,2,4,128]{3,0,2,1:T(8,128)(2,1)S(1)}, u32[]{:S(2)}, u32[]{:S(2)}) collective-permute-start(bf16[16,2,4,128]{3,0,2,1:T(8,128)(2,1)S(1)} %copy.67), channel_id=1, source_target_pairs={{124,0},{0,4},{4,8},{8,12},{12,16},{16,20},{20,24},{24,28},{28,32}... | collective-permute-start | bytes 98312 | tf_op jit(solution)/shard_map/while/body/eval_jaxpr/ppermute | solution.py:14
  737.3 24.2 %collective-permute-start.4 = (f32[16,2,4,128]{3,0,2,1:T(8,128)S(1)}, f32[16,2,4,128]{3,0,2,1:T(8,128)S(1)}, u32[]{:S(2)}, u32[]{:S(2)}) collective-permute-start(f32[16,2,4,128]{3,0,2,1:T(8,128)S(1)} %fusion.40), channel_id=1, source_target_pairs={{124,0},{0,4},{4,8},{8,12},{12,16},{16,20},{20,24},{24,28},{28,32}... | collective-permute-start | bytes 196616 | tf_op jit(solution)/shard_map/while/body/eval_jaxpr/ppermute | solution.py:14
  739.2 22.3 %collective-permute-start = (bf16[16,2,4,128]{3,0,2,1:T(8,128)(2,1)S(1)}, bf16[16,2,4,128]{3,0,2,1:T(8,128)(2,1)S(1)}, u32[]{:S(2)}, u32[]{:S(2)}) collective-permute-start(bf16[16,2,4,128]{3,0,2,1:T(8,128)(2,1)S(1)} %copy.67), channel_id=1, source_target_pairs={{124,0},{0,4},{4,8},{8,12},{12,16},{16,20},{20,24},{24,28},{28,32}... | collective-permute-start | bytes 98312 | tf_op jit(solution)/shard_map/while/body/eval_jaxpr/ppermute | solution.py:14
  (131 other events, 1675.4 us)
where the time goes:
time: 868 us; the launch traced here: 861 us
  starting transfers between devices  426 us (49%)
  waiting for transfers between devices  251 us (29%)
  blocking collectives  74.4 us (9%)
  local copies, waits for them, and re-layouts  48 us (6%)
  loops' own time  25 us (3%)
  matrix products  24.6 us (3%)
  other arithmetic  11.8 us (1%)
    ppermute x160, starting transfers between devices, shifted(): return lax.ppermute(block, axis, route)  426 us
    ppermute x160, waiting for transfers between devices, shifted(): return lax.ppermute(block, axis, route)  251 us
    all_gather x3, blocking collectives, merged(): pieces = jax.tree.map(lambda part: lax.all_gather(part, axis), value)  74.4 us
    dynamic_slice x32, local copies, waits for them, and re-layouts, cycle_turn(): tile_bit = lax.dynamic_slice(tile_mask, (tile, my_tile), (1, 1))[0, 0]  42.9 us
    another operation x1, loops' own time, per_device(): carry = lax.fori_loop(0, blocks, cycle_turn, carry)  24.9 us
  transfers between devices with their start and end apart: 160, of which 48 were waited for; matrix products, arithmetic and copies ran while one was open for 0% of the time, Pallas kernels for 0%

commit v1 on v0

v1 whole, which is shorter than its diff:
```python
import math

import jax
import jax.numpy as jnp
from jax import lax
from jax.experimental import pallas as pl
from jax.experimental.pallas import tpu as pltpu
from jax.sharding import PartitionSpec as P

HD = 128
LANES = 128
HIDDEN = -1e30
FLOOR = -1e29
RATE = math.log2(math.e) / math.sqrt(HD)
F32 = jnp.float32
BF16 = jnp.bfloat16
VMEM = pl.BlockSpec(memory_space=pltpu.VMEM)
SMEM = pl.BlockSpec(memory_space=pltpu.SMEM)


def lane_ids(rows):
    return lax.broadcasted_iota(jnp.int32, (rows, LANES), 1)


def row_ids(rows):
    return lax.broadcasted_iota(jnp.int32, (rows, LANES), 0)


def split3(x):
    first = x.astype(BF16).astype(F32)
    rest = x - first
    second = rest.astype(BF16).astype(F32)
    return first, second, (rest - second).astype(BF16).astype(F32)


def stats_block(top, total):
    parts = split3(top) + split3(total)
    rows = row_ids(16)
    block = jnp.zeros((16, LANES), F32)
    for number, part in enumerate(parts):
        block = jnp.where(rows == number, part, block)
    return block.astype(BF16)


def read_stats(block):
    block = block.astype(F32)
    top = block[0:1] + block[1:2] + block[2:3]
    total = block[3:4] + block[4:5] + block[5:6]
    return top, total


def pack_kernel(q_ref, bounds_ref, out_ref):
    heads = q_ref.shape[1] // HD
    rows = q_ref.shape[0]
    blocks = [q_ref[:, h * HD:(h + 1) * HD] for h in range(heads)]
    bounds = bounds_ref[...]
    lanes = lane_ids(rows)
    tail = jnp.zeros((rows, LANES), F32)
    for side in range(2):
        value = bounds[:, side:side + 1]
        pieces = (value >> 9, (value >> 1) & 255, value & 1)
        for number, piece in enumerate(pieces):
            tail = jnp.where(lanes == 3 * side + number, piece.astype(F32), tail)
    blocks.append(tail.astype(BF16))
    packed = jnp.concatenate(blocks, axis=0)
    for copy in range(out_ref.shape[0]):
        out_ref[copy] = packed


def project_kernel(x_ref, kw_ref, vw_ref, k_ref, v_ref, k_acc, v_acc):
    step = pl.program_id(0)

    @pl.when(step == 0)
    def _():
        k_acc[...] = jnp.zeros_like(k_acc)
        v_acc[...] = jnp.zeros_like(v_acc)

    x = x_ref[...]
    k_acc[...] += jnp.dot(x, kw_ref[...], preferred_element_type=F32)
    v_acc[...] += jnp.dot(x, vw_ref[...], preferred_element_type=F32)

    @pl.when(step == pl.num_programs(0) - 1)
    def _():
        k_ref[...] = k_acc[...].astype(BF16)
        v_ref[...] = v_acc[...].astype(BF16)


def attend_kernel(bits_ref, start_ref, q_ref, k_ref, v_ref, out_ref):
    tiles = q_ref.shape[0]
    vis = k_ref.shape[0]
    kv_heads = k_ref.shape[1] // HD
    text = 16
    group_rows = LANES // kv_heads
    columns = (lax.broadcasted_iota(jnp.int32, (text, vis), 1) + start_ref[0]).astype(F32)

    def tile_step(t, _):
        @pl.when(bits_ref[t] == 1)
        def _():
            edges = q_ref[t, LANES:, :].astype(F32)
            lower = edges[:, 0:1] * 512 + edges[:, 1:2] * 2 + edges[:, 2:3]
            upper = edges[:, 3:4] * 512 + edges[:, 4:5] * 2 + edges[:, 5:6]
            visible = (columns >= lower) & (columns < upper)
            bias = jnp.where(visible, 0.0, HIDDEN)
            tops, totals = [], []
            for kv in range(kv_heads):
                rows = slice(kv * group_rows, (kv + 1) * group_rows)
                heads = slice(kv * HD, (kv + 1) * HD)
                scores = lax.dot_general(
                    q_ref[t, rows, :], k_ref[:, heads], (((1,), (1,)), ((), ())),
                    preferred_element_type=F32,
                )
                scores = (scores.reshape(group_rows // text, text, vis) + bias[None]).reshape(
                    group_rows, vis
                )
                top = jnp.maximum(jnp.max(scores, axis=1, keepdims=True), FLOOR)
                weights = jnp.exp2((scores - top) * RATE)
                totals.append(jnp.sum(weights, axis=1, keepdims=True))
                tops.append(top)
                summed = jnp.dot(
                    weights.astype(BF16), v_ref[:, heads], preferred_element_type=F32
                )
                out_ref[t, rows, :] = summed.astype(BF16)
            lanes = lane_ids(LANES)
            top = jnp.concatenate(tops, axis=0)
            total = jnp.concatenate(totals, axis=0)
            both = jnp.where(lanes == 0, top, jnp.where(lanes == 1, total, 0.0)).T
            out_ref[t, LANES:, :] = stats_block(both[0:1], both[1:2])

        @pl.when(bits_ref[t] != 1)
        def _():
            out_ref[t, :LANES, :] = jnp.zeros((LANES, LANES), BF16)
            out_ref[t, LANES:, :] = stats_block(
                jnp.full((1, LANES), FLOOR, F32), jnp.zeros((1, LANES), F32)
            )

        return 0

    lax.fori_loop(0, tiles, tile_step, 0)


def joined(ref):
    n = ref.shape[0]
    stats = [read_stats(ref[s, LANES:, :]) for s in range(n)]
    tops = jnp.concatenate([top for top, _ in stats], axis=0)
    totals = jnp.concatenate([total for _, total in stats], axis=0)
    top = jnp.max(tops, axis=0, keepdims=True)
    factors = jnp.exp2((tops - top) * RATE)
    total = jnp.sum(factors * totals, axis=0, keepdims=True)
    padded = jnp.concatenate([factors, total, jnp.zeros((LANES - n - 1, LANES), F32)], axis=0).T
    summed = jnp.zeros((LANES, LANES), F32)
    for s in range(n):
        summed += padded[:, s:s + 1] * ref[s, :LANES, :].astype(F32)
    return top, total, padded[:, n:n + 1], summed


def join_kernel(in_ref, out_ref):
    top, total, _, summed = joined(in_ref)
    piece = jnp.concatenate([summed.astype(BF16), stats_block(top, total)], axis=0)
    for copy in range(out_ref.shape[0]):
        out_ref[copy] = piece


def finish_kernel(in_ref, out_ref):
    _, _, total, summed = joined(in_ref)
    result = (summed / total).astype(BF16)
    rows = out_ref.shape[0]
    for h in range(out_ref.shape[1] // HD):
        out_ref[:, h * HD:(h + 1) * HD] = result[h * rows:(h + 1) * rows]


def per_device(visual, key_weight, value_weight, queries, bounds, tile_mask):
    vis_rows, depth = visual.shape
    width = key_weight.shape[1]
    text_rows = queries.shape[0]
    blocks = lax.axis_size("blk")
    phases = lax.axis_size("phase")
    my_tile = lax.axis_index("phase") * blocks + lax.axis_index("blk")
    piece_rows = LANES + 16

    def exchange(pieces, axis):
        return lax.all_to_all(pieces, axis, 0, 0, tiled=True)

    packed = pl.pallas_call(
        pack_kernel,
        out_shape=jax.ShapeDtypeStruct((blocks, piece_rows, LANES), BF16),
        in_specs=[VMEM, VMEM],
        out_specs=VMEM,
    )(queries, bounds)
    gathered = exchange(packed, "blk")

    chunk = 512
    keys, values = pl.pallas_call(
        project_kernel,
        grid=(depth // chunk,),
        in_specs=[
            pl.BlockSpec((vis_rows, chunk), lambda i: (0, i)),
            pl.BlockSpec((chunk, width), lambda i: (i, 0)),
            pl.BlockSpec((chunk, width), lambda i: (i, 0)),
        ],
        out_specs=[pl.BlockSpec((vis_rows, width), lambda i: (0, 0))] * 2,
        out_shape=[jax.ShapeDtypeStruct((vis_rows, width), BF16)] * 2,
        scratch_shapes=[pltpu.VMEM((vis_rows, width), F32)] * 2,
        compiler_params=pltpu.CompilerParams(dimension_semantics=("arbitrary",)),
        cost_estimate=pl.CostEstimate(
            flops=4 * vis_rows * depth * width,
            bytes_accessed=2 * depth * (vis_rows + 2 * width),
            transcendentals=0,
        ),
    )(visual, key_weight, value_weight)

    tile_ids = lax.broadcasted_iota(jnp.int32, tile_mask.shape, 1)
    bits = jnp.sum(jnp.where(tile_ids == my_tile, tile_mask, 0), axis=1)
    start = (my_tile * vis_rows).astype(jnp.int32).reshape(1)
    partials = pl.pallas_call(
        attend_kernel,
        out_shape=jax.ShapeDtypeStruct((blocks, piece_rows, LANES), BF16),
        in_specs=[SMEM, SMEM, VMEM, VMEM, VMEM],
        out_specs=VMEM,
    )(bits, start, gathered, keys, values)

    partials = exchange(partials, "blk")
    section = pl.pallas_call(
        join_kernel,
        out_shape=jax.ShapeDtypeStruct((phases, piece_rows, LANES), BF16),
        in_specs=[VMEM],
        out_specs=VMEM,
    )(partials)
    sections = exchange(section, "phase")
    return pl.pallas_call(
        finish_kernel,
        out_shape=jax.ShapeDtypeStruct(queries.shape, BF16),
        in_specs=[VMEM],
        out_specs=VMEM,
    )(sections)


def solution(mesh):
    return jax.shard_map(
        per_device,
        mesh=mesh,
        in_specs=(
            P(("phase", "blk"), None),
            P(None, "head"),
            P(None, "head"),
            P("blk", "head"),
            P("blk", None),
            P(),
        ),
        out_specs=P("blk", "head"),
        check_vma=False,
    )
```

time: 868 us -> 140 us (0.16)
  the two profiles are of different devices: /device:TPU:8 before, /device:TPU:16 now
where the time goes in v1:
time: 140 us; the launch traced here: 139 us
  blocking collectives  57.8 us (41%)
  Pallas kernels  30.7 us (22%)
  waiting for transfers between devices  25.2 us (18%)
  starting transfers between devices  22.1 us (16%)
  local copies, waits for them, and re-layouts  2.41 us (2%)
    all_to_all x2, blocking collectives, exchange(): return lax.all_to_all(pieces, axis, 0, 0, tiled=True)  57.8 us
    all_to_all x1, waiting for transfers between devices, exchange(): return lax.all_to_all(pieces, axis, 0, 0, tiled=True)  25.2 us
    all_to_all x1, starting transfers between devices, exchange(): return lax.all_to_all(pieces, axis, 0, 0, tiled=True)  22.1 us
    pallas_call x1, Pallas kernels, per_device(): pl.pallas_call(attend_kernel, out_shape=jax.ShapeDtypeStruct((blocks, pie...  15.7 us
    pallas_call x1, Pallas kernels, per_device(): pl.pallas_call(project_kernel, grid=(depth // chunk,), in_specs=[pl.Block...  8.18 us
    pallas_call x1, Pallas kernels, per_device(): pl.pallas_call(join_kernel, out_shape=jax.ShapeDtypeStruct((phases, piece...  2.86 us
  transfers between devices with their start and end apart: 1, of which 1 were waited for; matrix products, arithmetic and copies ran while one was open for 0% of the time, Pallas kernels for 6%

profile of v1, /device:TPU:16, one launch (start us, length us, event | category | flops | bytes accessed | tf_op | source)
XLA Modules:
  0.0 138.8 jit_solution(15532906992418714154)
XLA Ops:
  0.0 1.4 copy.7.bounds_ref
  1.4 1.9 %shard_map.64 = bf16[32,144,128]{2,1,0:T(8,128)(2,1)} custom-call(bf16[16,1024]{1,0:T(8,128)(2,1)} %q_ref.1, s32[16,2]{1,0:T(8,128)} %copy.7.bounds_ref), custom_call_target="tpu_custom_call" | custom-call | tf_op jit(solution)/shard_map/pallas_call | solution.py:183
  3.3 0.0 copy-start.1
  3.3 22.1 %all-to-all-start = ((bf16[32,144,128]{2,1,0:T(8,128)(2,1)}), bf16[32,144,128]{2,1,0:T(8,128)(2,1)S(1)}, u32[]{:S(2)}, u32[]{:S(2)}) async-start(bf16[32,144,128]{2,1,0:T(8,128)(2,1)} %shard_map.64), calls=%async_computation | async-start | bytes 2359296 | tf_op jit(solution)/shard_map/all_to_all | solution.py:181
  25.4 0.0 copy-done.1
  25.4 0.6 select_reduce_fusion.bits_ref
  26.0 8.2 %shard_map.65 = (bf16[512,256]{1,0:T(8,128)(2,1)}, bf16[512,256]{1,0:T(8,128)(2,1)}) custom-call(bf16[512,4096]{1,0:T(8,128)(2,1)} %x_ref.1, bf16[4096,256]{1,0:T(8,128)(2,1)} %kw_ref.1, bf16[4096,256]{1,0:T(8,128)(2,1)} %vw_ref.1), custom_call_target="tpu_custom_call" | custom-call | flops 2147483648 | bytes 8388608 | tf_op jit(solution)/shard_map/pallas_call | solution.py:192
  34.2 25.2 %all-to-all-done.q_ref = bf16[32,144,128]{2,1,0:T(8,128)(2,1)S(1)} async-done(((bf16[32,144,128]{2,1,0:T(8,128)(2,1)}), bf16[32,144,128]{2,1,0:T(8,128)(2,1)S(1)}, u32[]{:S(2)}, u32[]{:S(2)}) %all-to-all-start) | async-done | bytes 1179680 | tf_op jit(solution)/shard_map/all_to_all | solution.py:181
  59.4 0.0 copy-start
  59.4 1.1 copy-done
  60.5 15.7 %shard_map.66 = bf16[32,144,128]{2,1,0:T(8,128)(2,1)} custom-call(s32[32]{0:T(128)} %select_reduce_fusion.bits_ref, s32[1]{0:T(128)} %bitcast.start_ref, bf16[32,144,128]{2,1,0:T(8,128)(2,1)} %copy-done, bf16[512,256]{1,0:T(8,128)(2,1)} %get-tuple-element.7.k_ref, bf16[512,256]{1,0:T(8,128)(2,1)} %get-tuple-element.8.v_ref), custom_call_target="tpu_custom_call" | custom-call | tf_op jit(solution)/shard_map/pallas_call | solution.py:214
  76.2 40.6 %all_to_all.15.in_ref = bf16[32,144,128]{2,1,0:T(8,128)(2,1)} all-to-all(bf16[32,144,128]{2,1,0:T(8,128)(2,1)} %shard_map.66), channel_id=1, replica_groups=mesh['phase'=8,'blk'=32,'head'=4] {'blk'}, dimensions={0} | all-to-all | bytes 2359296 | tf_op jit(solution)/shard_map/all_to_all | solution.py:181
  116.8 2.9 %shard_map.67 = bf16[8,144,128]{2,1,0:T(8,128)(2,1)} custom-call(bf16[32,144,128]{2,1,0:T(8,128)(2,1)} %all_to_all.15.in_ref), custom_call_target="tpu_custom_call" | custom-call | tf_op jit(solution)/shard_map/pallas_call | solution.py:222
  119.7 17.2 %all_to_all.16.in_ref = bf16[8,144,128]{2,1,0:T(8,128)(2,1)} all-to-all(bf16[8,144,128]{2,1,0:T(8,128)(2,1)} %shard_map.67), channel_id=1, replica_groups=mesh['phase'=8,'blk'=32,'head'=4] {'phase'}, dimensions={0} | all-to-all | bytes 589824 | tf_op jit(solution)/shard_map/all_to_all | solution.py:181
  136.9 2.0 %shard_map.68 = bf16[16,1024]{1,0:T(8,128)(2,1)} custom-call(bf16[8,144,128]{2,1,0:T(8,128)(2,1)} %all_to_all.16.in_ref), custom_call_target="tpu_custom_call" | custom-call | tf_op jit(solution)/shard_map/pallas_call | solution.py:229
  (1 shorter events, 0.0 us)
Async XLA Ops:
  3.3 22.1 %copy-start.1 = (s32[32,256]{1,0:T(8,128)S(1)}, s32[32,256]{1,0:T(8,128)}, u32[]{:S(2)}) copy-start(s32[32,256]{1,0:T(8,128)} %param.11) | copy-start | bytes 98308
  3.3 56.2 %all-to-all-start = ((bf16[32,144,128]{2,1,0:T(8,128)(2,1)}), bf16[32,144,128]{2,1,0:T(8,128)(2,1)S(1)}, u32[]{:S(2)}, u32[]{:S(2)}) async-start(bf16[32,144,128]{2,1,0:T(8,128)(2,1)} %shard_map.64), calls=%async_computation | async-start | bytes 2359296 | tf_op jit(solution)/shard_map/all_to_all | solution.py:181
  59.4 1.1 copy-start

commit v2 on v1

v2 whole, which is shorter than its diff:
```python
import math

import jax
import jax.numpy as jnp
from jax import lax
from jax.experimental import pallas as pl
from jax.experimental.pallas import tpu as pltpu
from jax.sharding import PartitionSpec as P

HD = 128
LANES = 128
HIDDEN = -1e30
FLOOR = -1e29
RATE = math.log2(math.e) / math.sqrt(HD)
F32 = jnp.float32
BF16 = jnp.bfloat16
VMEM = pl.BlockSpec(memory_space=pltpu.VMEM)
SMEM = pl.BlockSpec(memory_space=pltpu.SMEM)


def lane_ids(rows):
    return lax.broadcasted_iota(jnp.int32, (rows, LANES), 1)


def row_ids(rows):
    return lax.broadcasted_iota(jnp.int32, (rows, LANES), 0)


def split3(x):
    first = x.astype(BF16).astype(F32)
    rest = x - first
    second = rest.astype(BF16).astype(F32)
    return first, second, (rest - second).astype(BF16).astype(F32)


def stats_block(top, total):
    parts = split3(top) + split3(total)
    rows = row_ids(16)
    block = jnp.zeros((16, LANES), F32)
    for number, part in enumerate(parts):
        block = jnp.where(rows == number, part, block)
    return block.astype(BF16)


def read_stats(block):
    block = block.astype(F32)
    top = block[0:1] + block[1:2] + block[2:3]
    total = block[3:4] + block[4:5] + block[5:6]
    return top, total


def pack_kernel(side_ref, q_ref, bounds_ref, out_ref):
    rows = q_ref.shape[0]
    width = q_ref.shape[1] // 2
    first = side_ref[0] * width
    blocks = [
        q_ref[:, pl.ds(pl.multiple_of(first + g * HD, HD), HD)] for g in range(width // HD)
    ]
    bounds = bounds_ref[...]
    lanes = lane_ids(rows)
    tail = jnp.zeros((rows, LANES), F32)
    for side in range(2):
        value = bounds[:, side:side + 1]
        pieces = (value >> 9, (value >> 1) & 255, value & 1)
        for number, piece in enumerate(pieces):
            tail = jnp.where(lanes == 3 * side + number, piece.astype(F32), tail)
    blocks.append(tail.astype(BF16))
    packed = jnp.concatenate(blocks, axis=0)
    for copy in range(out_ref.shape[0]):
        out_ref[copy] = packed


def project_kernel(side_ref, x_ref, kw_ref, vw_ref, keep_ref, send_ref, k_acc, v_acc):
    step = pl.program_id(0)

    @pl.when(step == 0)
    def _():
        k_acc[...] = jnp.zeros_like(k_acc)
        v_acc[...] = jnp.zeros_like(v_acc)

    x = x_ref[...]
    k_acc[...] += jnp.dot(x, kw_ref[...], preferred_element_type=F32)
    v_acc[...] += jnp.dot(x, vw_ref[...], preferred_element_type=F32)

    for side in range(2):
        @pl.when((step == pl.num_programs(0) - 1) & (side_ref[0] == side))
        def _():
            for head, out_ref in ((side, keep_ref), (1 - side, send_ref)):
                columns = slice(head * HD, (head + 1) * HD)
                out_ref[0] = k_acc[:, columns].astype(BF16)
                out_ref[1] = v_acc[:, columns].astype(BF16)


def attend_kernel(tiles_ref, bits_ref, q_ref, own_ref, other_ref, out_ref):
    pairs, _, piece, _ = q_ref.shape
    text = 16
    rows = piece - text
    group = rows // text
    vis = own_ref.shape[1]
    columns = lax.broadcasted_iota(jnp.int32, (text, vis), 1).astype(F32)

    def pair_step(pair, _):
        edges = []
        for half in range(2):
            digits = q_ref[pair, half, rows:, :].astype(F32)
            lower = digits[:, 0:1] * 512 + digits[:, 1:2] * 2 + digits[:, 2:3]
            upper = digits[:, 3:4] * 512 + digits[:, 4:5] * 2 + digits[:, 5:6]
            edges.append((lower, upper))
        queries = jnp.concatenate([q_ref[pair, half, :rows, :] for half in range(2)], axis=0)
        scores, tops = [], []
        for source, kv_ref in enumerate((own_ref, other_ref)):
            start = (tiles_ref[source] * vis).astype(F32)
            found = lax.dot_general(
                queries, kv_ref[0], (((1,), (1,)), ((), ())), preferred_element_type=F32
            ).reshape(2, group, text, vis)
            parts = []
            for half in range(2):
                lower, upper = edges[half]
                bit = bits_ref[source, 2 * pair + half]
                hidden = (1 - bit).astype(F32) * 1e7
                visible = (columns >= lower - start + hidden) & (columns < upper - start)
                bias = jnp.where(visible, 0.0, HIDDEN)
                parts.append(found[half] + bias[None])
            masked = jnp.stack(parts).reshape(2 * rows, vis)
            scores.append(masked)
            tops.append(jnp.max(masked, axis=1, keepdims=True))
        top = jnp.maximum(jnp.maximum(tops[0], tops[1]), FLOOR)
        total = jnp.zeros((2 * rows, 1), F32)
        summed = jnp.zeros((2 * rows, HD), F32)
        for masked, kv_ref in zip(scores, (own_ref, other_ref)):
            weights = jnp.exp2((masked - top) * RATE)
            total += jnp.sum(weights, axis=1, keepdims=True)
            summed += jnp.dot(weights.astype(BF16), kv_ref[1], preferred_element_type=F32)
        out_ref[pair, :LANES, :] = summed.astype(BF16)
        lanes = lane_ids(LANES)
        both = jnp.where(lanes == 0, top, jnp.where(lanes == 1, total, 0.0)).T
        out_ref[pair, LANES:, :] = stats_block(both[0:1], both[1:2])
        return 0

    lax.fori_loop(0, pairs, pair_step, 0, unroll=2)


def joined(pieces):
    n = len(pieces)
    rows = pieces[0].shape[0] - 16
    stats = [read_stats(piece[rows:, :]) for piece in pieces]
    tops = jnp.concatenate([top for top, _ in stats], axis=0)
    totals = jnp.concatenate([total for _, total in stats], axis=0)
    top = jnp.max(tops, axis=0, keepdims=True)
    factors = jnp.exp2((tops - top) * RATE)
    total = jnp.sum(factors * totals, axis=0, keepdims=True)
    spread = jnp.concatenate([factors, total, jnp.zeros((LANES - n - 1, LANES), F32)], axis=0).T
    summed = jnp.zeros((rows, LANES), F32)
    for s in range(n):
        summed += spread[:rows, s:s + 1] * pieces[s][:rows, :].astype(F32)
    return top, total, spread[:rows, n:n + 1], summed


def join_pairs_kernel(in_ref, out_ref):
    sources, pairs = in_ref.shape[:2]
    rows = out_ref.shape[1] - 16
    for pair in range(pairs):
        top, total, _, summed = joined([in_ref.at[s, pair] for s in range(sources)])
        summed = summed.astype(BF16)
        for half in range(2):
            cut = slice(half * rows, (half + 1) * rows)
            out_ref[2 * pair + half, :rows, :] = summed[cut]
            if half == 0:
                stats = stats_block(top, total)
            else:
                stats = stats_block(pltpu.roll(top, rows, 1), pltpu.roll(total, rows, 1))
            out_ref[2 * pair + half, rows:, :] = stats


def join_kernel(in_ref, out_ref):
    top, total, _, summed = joined([in_ref.at[s] for s in range(in_ref.shape[0])])
    piece = jnp.concatenate([summed.astype(BF16), stats_block(top, total)], axis=0)
    for copy in range(out_ref.shape[0]):
        out_ref[copy] = piece


def finish_kernel(in_ref, out_ref):
    sources = in_ref.shape[0]
    text = out_ref.shape[0]
    for side in range(2):
        _, _, total, summed = joined([in_ref.at[s] for s in range(side, sources, 2)])
        result = (summed / total).astype(BF16)
        group = result.shape[0] // text
        for g in range(group):
            first = (side * group + g) * HD
            out_ref[:, first:first + HD] = result[g * text:(g + 1) * text]


def call(kernel, out, in_specs):
    return pl.pallas_call(
        kernel, out_shape=jax.ShapeDtypeStruct(out, BF16), in_specs=in_specs, out_specs=VMEM
    )


def per_device(visual, key_weight, value_weight, queries, bounds, tile_mask):
    vis_rows, depth = visual.shape
    width = key_weight.shape[1]
    text = queries.shape[0]
    rows = queries.shape[1] // HD // 2 * text
    piece = rows + text
    zs, ys = lax.axis_size("zh"), lax.axis_size("y")
    phases = lax.axis_size("xh") * 2
    side = lax.axis_index("xl")
    blk = lax.axis_index("zh") * ys + lax.axis_index("y")
    phase = lax.axis_index("xh") * 2 + side
    tiles = jnp.stack([phase * (zs * ys) + blk, (phase ^ 1) * (zs * ys) + blk])
    side = side.reshape(1)

    def exchange(pieces, axis):
        return lax.all_to_all(pieces, axis, 0, 0, tiled=True)

    packed = call(pack_kernel, (zs, piece, LANES), [SMEM, VMEM, VMEM])(side, queries, bounds)
    column = exchange(packed, "zh")
    gathered = exchange(jnp.broadcast_to(column[None], (ys,) + column.shape), "y")

    chunk = 512
    half = pl.BlockSpec((2, vis_rows, HD), lambda i: (0, 0, 0))
    keep, send = pl.pallas_call(
        project_kernel,
        grid=(depth // chunk,),
        in_specs=[
            SMEM,
            pl.BlockSpec((vis_rows, chunk), lambda i: (0, i)),
            pl.BlockSpec((chunk, width), lambda i: (i, 0)),
            pl.BlockSpec((chunk, width), lambda i: (i, 0)),
        ],
        out_specs=[half, half],
        out_shape=[jax.ShapeDtypeStruct((2, vis_rows, HD), BF16)] * 2,
        scratch_shapes=[pltpu.VMEM((vis_rows, width), F32)] * 2,
        compiler_params=pltpu.CompilerParams(dimension_semantics=("arbitrary",)),
        cost_estimate=pl.CostEstimate(
            flops=4 * vis_rows * depth * width,
            bytes_accessed=2 * depth * (vis_rows + 2 * width),
            transcendentals=0,
        ),
    )(side, visual, key_weight, value_weight)
    other = lax.ppermute(send, "xl", [(0, 1), (1, 0)])

    tile_ids = lax.broadcasted_iota(jnp.int32, tile_mask.shape, 1)
    bits = jnp.stack([jnp.sum(jnp.where(tile_ids == tiles[s], tile_mask, 0), axis=1) for s in (0, 1)])
    bits = bits.reshape(2, zs, ys).swapaxes(1, 2).reshape(2, zs * ys)
    pairs = ys * zs // 2
    partials = call(attend_kernel, (pairs, LANES + 16, LANES), [SMEM, SMEM, VMEM, VMEM, VMEM])(
        tiles, bits, gathered.reshape(pairs, 2, piece, LANES), keep, other
    )
    partials = exchange(partials, "y").reshape(ys, zs // 2, LANES + 16, LANES)
    partials = call(join_pairs_kernel, (zs, piece, LANES), [VMEM])(partials)
    partials = exchange(partials, "zh")
    partials = call(join_kernel, (phases, piece, LANES), [VMEM])(partials)
    partials = exchange(partials, ("xh", "xl"))
    return call(finish_kernel, queries.shape, [VMEM])(partials)


def solution(mesh):
    phases, blocks, heads = (mesh.shape[name] for name in ("phase", "blk", "head"))
    fine = jax.sharding.Mesh(
        mesh.devices.reshape(phases // 2, 2, blocks // 8, 8, heads), ("xh", "xl", "zh", "y", "head")
    )
    phase, blk = ("xh", "xl"), ("zh", "y")
    return jax.shard_map(
        per_device,
        mesh=fine,
        in_specs=(
            P(phase + blk, None),
            P(None, "head"),
            P(None, "head"),
            P(blk, "head"),
            P(blk, None),
            P(),
        ),
        out_specs=P(blk, "head"),
        check_vma=False,
    )
```

time: 140 us -> 120 us (0.86)
  waiting for transfers between devices: 25.2 us -> 3.89 us
  blocking collectives: 57.8 us -> 73.9 us
  starting transfers between devices: 22.1 us -> 11.3 us
  Pallas kernels: 30.7 us -> 24.5 us
  local copies, waits for them, and re-layouts: 2.41 us -> 4.02 us
    all_to_all x1, waiting for transfers between devices: 25.2 us -> 0.5 us  [exchange(): return lax.all_to_all(pieces, axis, 0, 0, tiled=True)]
    all_to_all x2 -> x4, blocking collectives: 57.8 us -> 73.9 us  [exchange(): return lax.all_to_all(pieces, axis, 0, 0, tiled=True)]
    all_to_all x1, starting transfers between devices: 22.1 us -> 7.89 us  [exchange(): return lax.all_to_all(pieces, axis, 0, 0, tiled=True)]
    pallas_call x5 -> x6, Pallas kernels: 30.7 us -> 24.5 us  [the longest x1 9.06 us: per_device(): call(attend_kernel, (pairs, LANES + 16, LANES), [SMEM, SMEM, VMEM, VMEM,...]
    ppermute x0 -> x1, waiting for transfers between devices: none -> 3.4 us  [per_device(): other = lax.ppermute(send, 'xl', [(0, 1), (1, 0)])]
    ppermute x0 -> x1, starting transfers between devices: none -> 3.39 us  [per_device(): other = lax.ppermute(send, 'xl', [(0, 1), (1, 0)])]
  transfers between devices with their start and end apart: 1 -> 2, of which waited for: 1 -> 2; matrix products, arithmetic and copies ran while one was open for 0% -> 1% of each run, Pallas kernels for 6% -> 7%
where the time goes in v2:
time: 120 us; the launch traced here: 118 us
  blocking collectives  73.9 us (62%)
  Pallas kernels  24.5 us (20%)
  starting transfers between devices  11.3 us (9%)
  local copies, waits for them, and re-layouts  4.02 us (3%)
  waiting for transfers between devices  3.89 us (3%)
    all_to_all x4, blocking collectives, exchange(): return lax.all_to_all(pieces, axis, 0, 0, tiled=True)  73.9 us
    pallas_call x1, Pallas kernels, per_device(): call(attend_kernel, (pairs, LANES + 16, LANES), [SMEM, SMEM, VMEM, VMEM,...  9.06 us
    pallas_call x1, Pallas kernels, per_device(): pl.pallas_call(project_kernel, grid=(depth // chunk,), in_specs=[SMEM, pl...  8.24 us
    all_to_all x1, starting transfers between devices, exchange(): return lax.all_to_all(pieces, axis, 0, 0, tiled=True)  7.89 us
    ppermute x1, waiting for transfers between devices, per_device(): other = lax.ppermute(send, 'xl', [(0, 1), (1, 0)])  3.4 us
    ppermute x1, starting transfers between devices, per_device(): other = lax.ppermute(send, 'xl', [(0, 1), (1, 0)])  3.39 us
  transfers between devices with their start and end apart: 2, of which 2 were waited for; matrix products, arithmetic and copies ran while one was open for 1% of the time, Pallas kernels for 7%

profile of v2, /device:TPU:16, one launch (start us, length us, event | category | flops | bytes accessed | tf_op | source)
XLA Modules:
  0.0 118.4 jit_solution(637516604022467053)
XLA Ops:
  0.0 1.4 %copy.10.bounds_ref = s32[16,2]{1,0:T(8,128)} copy(s32[16,2]{0,1:T(2,128)} %param.10) | data formatting | bytes 256 | tf_op args[4]
  1.4 1.5 %shard_map.64 = bf16[4,80,128]{2,1,0:T(8,128)(2,1)} custom-call(s32[1]{0:T(128)} %bitcast.3.side_ref, bf16[16,1024]{1,0:T(8,128)(2,1)} %q_ref.1, s32[16,2]{1,0:T(8,128)} %copy.10.bounds_ref), custom_call_target="tpu_custom_call" | custom-call | tf_op jit(solution)/shard_map/pallas_call | solution.py:217
  2.8 24.1 %all_to_all.25 = bf16[4,80,128]{2,1,0:T(8,128)(2,1)S(1)} all-to-all(bf16[4,80,128]{2,1,0:T(8,128)(2,1)} %shard_map.64), channel_id=1, replica_groups=mesh['xh'=4,'xl'=2,'zh'=4,'y'=8,'head'=4] {'zh'}, dimensions={0} | all-to-all | bytes 163840 | tf_op jit(solution)/shard_map/all_to_all | solution.py:215
  26.9 0.9 broadcast_in_dim.12
  27.8 7.9 %all-to-all-start.1 = ((bf16[8,4,80,128]{3,2,1,0:T(8,128)(2,1)}), bf16[8,4,80,128]{3,2,1,0:T(8,128)(2,1)S(1)}, u32[]{:S(2)}, u32[]{:S(2)}) async-start(bf16[8,4,80,128]{3,2,1,0:T(8,128)(2,1)} %broadcast_in_dim.12), calls=%async_computation.1 | async-start | bytes 1310720 | tf_op jit(solution)/shard_map/all_to_all | solution.py:215
  35.7 0.0 copy-start.2
  35.7 8.2 %shard_map.65 = (bf16[2,512,128]{2,1,0:T(8,128)(2,1)}, bf16[2,512,128]{2,1,0:T(8,128)(2,1)}) custom-call(s32[1]{0:T(128)} %bitcast.3.side_ref, bf16[512,4096]{1,0:T(8,128)(2,1)} %x_ref.1, bf16[4096,256]{1,0:T(8,128)(2,1)} %kw_ref.1, bf16[4096,256]{1,0:T(8,128)(2,1)} %vw_ref.1), custom_call_target="tpu_custom_call" | custom-call | flops 2147483648 | bytes 8388608 | tf_op jit(solution)/shard_map/pallas_call | solution.py:223
  44.0 3.4 %collective-permute-start = (bf16[2,512,128]{2,1,0:T(8,128)(2,1)}, bf16[2,512,128]{2,1,0:T(8,128)(2,1)S(1)}, u32[]{:S(2)}, u32[]{:S(2)}) collective-permute-start(bf16[2,512,128]{2,1,0:T(8,128)(2,1)} %get-tuple-element.8), channel_id=1, source_target_pairs={{0,128},{128,0},{1,129},{129,1},{2,130},{130,2},{3,131},{131,3},{4... | collective-permute-start | bytes 786440 | tf_op jit(solution)/shard_map/ppermute | solution.py:242
  47.4 0.0 copy-done.2
  47.4 0.1 select_reduce_fusion.1
  47.5 0.1 stack.22
  47.6 0.1 stack.21
  47.7 0.1 copy.9
  47.8 0.7 reshape.18.bits_ref
  48.4 0.6 pad_add_fusion.tiles_ref
  49.0 3.4 %collective-permute-done.other_ref = bf16[2,512,128]{2,1,0:T(8,128)(2,1)S(1)} collective-permute-done((bf16[2,512,128]{2,1,0:T(8,128)(2,1)}, bf16[2,512,128]{2,1,0:T(8,128)(2,1)S(1)}, u32[]{:S(2)}, u32[]{:S(2)}) %collective-permute-start) | collective-permute-done | bytes 262176 | tf_op jit(solution)/shard_map/ppermute | solution.py:242
  52.4 0.0 copy-start.1
  52.4 0.5 all-to-all-done.1
  52.9 0.0 copy-start
  52.9 0.2 copy-done.1
  53.1 0.6 copy-done
  53.8 9.1 %shard_map.66 = bf16[16,144,128]{2,1,0:T(8,128)(2,1)} custom-call(s32[2]{0:T(128)} %pad_add_fusion.tiles_ref, s32[2,32]{1,0:T(2,128)} %reshape.18.bits_ref, bf16[16,2,80,128]{3,2,1,0:T(8,128)(2,1)} %bitcast.7, bf16[2,512,128]{2,1,0:T(8,128)(2,1)} %get-tuple-element.7.own_ref, bf16[2,512,128]{2,1,0:T(8,128)(2,1)} %copy-done.1), custom_call_target="tpu_custom_call" | custom-call | tf_op jit(solution)/shard_map/pallas_call | solution.py:248
  62.8 21.2 %all_to_all.26 = bf16[16,144,128]{2,1,0:T(8,128)(2,1)} all-to-all(bf16[16,144,128]{2,1,0:T(8,128)(2,1)} %shard_map.66), channel_id=1, replica_groups=mesh['xh'=4,'xl'=2,'zh'=4,'y'=8,'head'=4] {'y'}, dimensions={0} | all-to-all | bytes 1179648 | tf_op jit(solution)/shard_map/all_to_all | solution.py:215
  84.1 2.2 %shard_map.67 = bf16[4,80,128]{2,1,0:T(8,128)(2,1)} custom-call(bf16[8,2,144,128]{3,2,1,0:T(8,128)(2,1)} %bitcast.8), custom_call_target="tpu_custom_call" | custom-call | tf_op jit(solution)/shard_map/pallas_call | solution.py:252
  86.3 12.3 %all_to_all.27.in_ref = bf16[4,80,128]{2,1,0:T(8,128)(2,1)} all-to-all(bf16[4,80,128]{2,1,0:T(8,128)(2,1)} %shard_map.67), channel_id=1, replica_groups=mesh['xh'=4,'xl'=2,'zh'=4,'y'=8,'head'=4] {'zh'}, dimensions={0} | all-to-all | bytes 163840 | tf_op jit(solution)/shard_map/all_to_all | solution.py:215
  98.6 1.8 %shard_map.68 = bf16[8,80,128]{2,1,0:T(8,128)(2,1)} custom-call(bf16[4,80,128]{2,1,0:T(8,128)(2,1)} %all_to_all.27.in_ref), custom_call_target="tpu_custom_call" | custom-call | tf_op jit(solution)/shard_map/pallas_call | solution.py:254
  100.3 16.3 %all_to_all.28.in_ref = bf16[8,80,128]{2,1,0:T(8,128)(2,1)} all-to-all(bf16[8,80,128]{2,1,0:T(8,128)(2,1)} %shard_map.68), channel_id=1, replica_groups=mesh['xh'=4,'xl'=2,'zh'=4,'y'=8,'head'=4] {'xh','xl'}, dimensions={0} | all-to-all | bytes 327680 | tf_op jit(solution)/shard_map/all_to_all | solution.py:215
  116.6 1.8 %shard_map.69 = bf16[16,1024]{1,0:T(8,128)(2,1)} custom-call(bf16[8,80,128]{2,1,0:T(8,128)(2,1)} %all_to_all.28.in_ref), custom_call_target="tpu_custom_call" | custom-call | tf_op jit(solution)/shard_map/pallas_call | solution.py:256
  (2 shorter events, 0.0 us)
Async XLA Ops:
  27.8 25.1 %all-to-all-start.1 = ((bf16[8,4,80,128]{3,2,1,0:T(8,128)(2,1)}), bf16[8,4,80,128]{3,2,1,0:T(8,128)(2,1)S(1)}, u32[]{:S(2)}, u32[]{:S(2)}) async-start(bf16[8,4,80,128]{3,2,1,0:T(8,128)(2,1)} %broadcast_in_dim.12), calls=%async_computation.1 | async-start | bytes 1310720 | tf_op jit(solution)/shard_map/all_to_all | solution.py:215
  35.7 11.7 %copy-start.2 = (s32[32,256]{1,0:T(8,128)S(1)}, s32[32,256]{1,0:T(8,128)}, u32[]{:S(2)}) copy-start(s32[32,256]{1,0:T(8,128)} %param.11) | copy-start | bytes 98308
  44.0 8.5 %collective-permute-start = (bf16[2,512,128]{2,1,0:T(8,128)(2,1)}, bf16[2,512,128]{2,1,0:T(8,128)(2,1)S(1)}, u32[]{:S(2)}, u32[]{:S(2)}) collective-permute-start(bf16[2,512,128]{2,1,0:T(8,128)(2,1)} %get-tuple-element.8), channel_id=1, source_target_pairs={{0,128},{128,0},{1,129},{129,1},{2,130},{130,2},{3,131},{131,3},{4... | collective-permute-start | bytes 786440 | tf_op jit(solution)/shard_map/ppermute | solution.py:242
  52.4 0.7 copy-start.1
  52.9 0.8 copy-start

commit v3 on v2

--- a/solution.py
+++ b/solution.py
@@ -14,6 +14,9 @@
 RATE = math.log2(math.e) / math.sqrt(HD)
 F32 = jnp.float32
 BF16 = jnp.bfloat16
+TOGETHER = 2
+UNROLL = 2
+GRANT = 24 << 20
 VMEM = pl.BlockSpec(memory_space=pltpu.VMEM)
 SMEM = pl.BlockSpec(memory_space=pltpu.SMEM)
 
@@ -56,11 +59,16 @@
     blocks = [
         q_ref[:, pl.ds(pl.multiple_of(first + g * HD, HD), HD)] for g in range(width // HD)
     ]
-    bounds = bounds_ref[...]
+    bounds = bounds_ref[...].astype(F32)
     lanes = lane_ids(rows)
     tail = jnp.zeros((rows, LANES), F32)
+    square = (rows, rows)
+    diagonal = lax.broadcasted_iota(jnp.int32, square, 0) == lax.broadcasted_iota(
+        jnp.int32, square, 1
+    )
     for side in range(2):
-        value = bounds[:, side:side + 1]
+        row = jnp.broadcast_to(bounds[side:side + 1, :], square)
+        value = jnp.sum(jnp.where(diagonal, row, 0.0), axis=1, keepdims=True).astype(jnp.int32)
         pieces = (value >> 9, (value >> 1) & 255, value & 1)
         for number, piece in enumerate(pieces):
             tail = jnp.where(lanes == 3 * side + number, piece.astype(F32), tail)
@@ -92,52 +100,61 @@
 
 
 def attend_kernel(tiles_ref, bits_ref, q_ref, own_ref, other_ref, out_ref):
-    pairs, _, piece, _ = q_ref.shape
+    tiles, piece, _ = q_ref.shape
     text = 16
     rows = piece - text
     group = rows // text
     vis = own_ref.shape[1]
+    together = TOGETHER
     columns = lax.broadcasted_iota(jnp.int32, (text, vis), 1).astype(F32)
 
-    def pair_step(pair, _):
+    def step(number, _):
+        first = number * together
         edges = []
-        for half in range(2):
-            digits = q_ref[pair, half, rows:, :].astype(F32)
+        for at in range(together):
+            digits = q_ref[first + at, rows:, :].astype(F32)
             lower = digits[:, 0:1] * 512 + digits[:, 1:2] * 2 + digits[:, 2:3]
             upper = digits[:, 3:4] * 512 + digits[:, 4:5] * 2 + digits[:, 5:6]
             edges.append((lower, upper))
-        queries = jnp.concatenate([q_ref[pair, half, :rows, :] for half in range(2)], axis=0)
+        queries = jnp.concatenate([q_ref[first + at, :rows, :] for at in range(together)], axis=0)
         scores, tops = [], []
         for source, kv_ref in enumerate((own_ref, other_ref)):
             start = (tiles_ref[source] * vis).astype(F32)
             found = lax.dot_general(
                 queries, kv_ref[0], (((1,), (1,)), ((), ())), preferred_element_type=F32
-            ).reshape(2, group, text, vis)
+            ).reshape(together, group, text, vis)
             parts = []
-            for half in range(2):
-                lower, upper = edges[half]
-                bit = bits_ref[source, 2 * pair + half]
-                hidden = (1 - bit).astype(F32) * 1e7
+            for at in range(together):
+                lower, upper = edges[at]
+                hidden = (1 - bits_ref[source, first + at]).astype(F32) * 1e7
                 visible = (columns >= lower - start + hidden) & (columns < upper - start)
                 bias = jnp.where(visible, 0.0, HIDDEN)
-                parts.append(found[half] + bias[None])
-            masked = jnp.stack(parts).reshape(2 * rows, vis)
+                parts.append(found[at] + bias[None])
+            masked = jnp.stack(parts).reshape(together * rows, vis)
             scores.append(masked)
             tops.append(jnp.max(masked, axis=1, keepdims=True))
         top = jnp.maximum(jnp.maximum(tops[0], tops[1]), FLOOR)
-        total = jnp.zeros((2 * rows, 1), F32)
-        summed = jnp.zeros((2 * rows, HD), F32)
+        total = jnp.zeros((together * rows, 1), F32)
+        summed = jnp.zeros((together * rows, HD), F32)
         for masked, kv_ref in zip(scores, (own_ref, other_ref)):
             weights = jnp.exp2((masked - top) * RATE)
             total += jnp.sum(weights, axis=1, keepdims=True)
             summed += jnp.dot(weights.astype(BF16), kv_ref[1], preferred_element_type=F32)
-        out_ref[pair, :LANES, :] = summed.astype(BF16)
+        summed = summed.astype(BF16)
         lanes = lane_ids(LANES)
-        both = jnp.where(lanes == 0, top, jnp.where(lanes == 1, total, 0.0)).T
-        out_ref[pair, LANES:, :] = stats_block(both[0:1], both[1:2])
+        for pair in range(together // 2):
+            cut = slice(pair * LANES, (pair + 1) * LANES)
+            both = jnp.where(lanes == 0, top[cut], jnp.where(lanes == 1, total[cut], 0.0)).T
+            both = both[0:8]
+            for half in range(2):
+                at = 2 * pair + half
+                out_ref[first + at, :rows, :] = summed[at * rows:(at + 1) * rows]
+                if half:
+                    both = pltpu.roll(both, rows, 1)
+                out_ref[first + at, rows:, :] = stats_block(both[0:1], both[1:2])
         return 0
 
-    lax.fori_loop(0, pairs, pair_step, 0, unroll=2)
+    lax.fori_loop(0, tiles // together, step, 0, unroll=UNROLL)
 
 
 def joined(pieces):
@@ -156,22 +173,6 @@
     return top, total, spread[:rows, n:n + 1], summed
 
 
-def join_pairs_kernel(in_ref, out_ref):
-    sources, pairs = in_ref.shape[:2]
-    rows = out_ref.shape[1] - 16
-    for pair in range(pairs):
-        top, total, _, summed = joined([in_ref.at[s, pair] for s in range(sources)])
-        summed = summed.astype(BF16)
-        for half in range(2):
-            cut = slice(half * rows, (half + 1) * rows)
-            out_ref[2 * pair + half, :rows, :] = summed[cut]
-            if half == 0:
-                stats = stats_block(top, total)
-            else:
-                stats = stats_block(pltpu.roll(top, rows, 1), pltpu.roll(total, rows, 1))
-            out_ref[2 * pair + half, rows:, :] = stats
-
-
 def join_kernel(in_ref, out_ref):
     top, total, _, summed = joined([in_ref.at[s] for s in range(in_ref.shape[0])])
     piece = jnp.concatenate([summed.astype(BF16), stats_block(top, total)], axis=0)
@@ -193,7 +194,8 @@
 
 def call(kernel, out, in_specs):
     return pl.pallas_call(
-        kernel, out_shape=jax.ShapeDtypeStruct(out, BF16), in_specs=in_specs, out_specs=VMEM
+        kernel, out_shape=jax.ShapeDtypeStruct(out, BF16), in_specs=in_specs, out_specs=VMEM,
+        compiler_params=pltpu.CompilerParams(vmem_limit_bytes=GRANT),
     )
 
 
@@ -214,9 +216,8 @@
     def exchange(pieces, axis):
         return lax.all_to_all(pieces, axis, 0, 0, tiled=True)
 
-    packed = call(pack_kernel, (zs, piece, LANES), [SMEM, VMEM, VMEM])(side, queries, bounds)
-    column = exchange(packed, "zh")
-    gathered = exchange(jnp.broadcast_to(column[None], (ys,) + column.shape), "y")
+    packed = call(pack_kernel, (zs * ys, piece, LANES), [SMEM, VMEM, VMEM])(side, queries, bounds.T)
+    gathered = exchange(packed, ("zh", "y"))
 
     chunk = 512
     half = pl.BlockSpec((2, vis_rows, HD), lambda i: (0, 0, 0))
@@ -232,7 +233,8 @@
         out_specs=[half, half],
         out_shape=[jax.ShapeDtypeStruct((2, vis_rows, HD), BF16)] * 2,
         scratch_shapes=[pltpu.VMEM((vis_rows, width), F32)] * 2,
-        compiler_params=pltpu.CompilerParams(dimension_semantics=("arbitrary",)),
+        compiler_params=pltpu.CompilerParams(dimension_semantics=("arbitrary",), vmem_limit_bytes=62 << 20
+        ),
         cost_estimate=pl.CostEstimate(
             flops=4 * vis_rows * depth * width,
             bytes_accessed=2 * depth * (vis_rows + 2 * width),
@@ -242,15 +244,11 @@
     other = lax.ppermute(send, "xl", [(0, 1), (1, 0)])
 
     tile_ids = lax.broadcasted_iota(jnp.int32, tile_mask.shape, 1)
-    bits = jnp.stack([jnp.sum(jnp.where(tile_ids == tiles[s], tile_mask, 0), axis=1) for s in (0, 1)])
-    bits = bits.reshape(2, zs, ys).swapaxes(1, 2).reshape(2, zs * ys)
-    pairs = ys * zs // 2
-    partials = call(attend_kernel, (pairs, LANES + 16, LANES), [SMEM, SMEM, VMEM, VMEM, VMEM])(
-        tiles, bits, gathered.reshape(pairs, 2, piece, LANES), keep, other
-    )
-    partials = exchange(partials, "y").reshape(ys, zs // 2, LANES + 16, LANES)
-    partials = call(join_pairs_kernel, (zs, piece, LANES), [VMEM])(partials)
-    partials = exchange(partials, "zh")
+    bits = jnp.sum(jnp.where(tile_ids[None] == tiles[:, None, None], tile_mask[None], 0), axis=2)
+    partials = call(attend_kernel, (zs * ys, piece, LANES), [SMEM, SMEM, VMEM, VMEM, VMEM])(
+        tiles, bits, gathered, keep, other
+    )
+    partials = exchange(partials, ("zh", "y"))
     partials = call(join_kernel, (phases, piece, LANES), [VMEM])(partials)
     partials = exchange(partials, ("xh", "xl"))
     return call(finish_kernel, queries.shape, [VMEM])(partials)

time: 120 us -> 103 us (0.86)
  blocking collectives: 73.9 us -> 44.5 us
  starting transfers between devices: 11.3 us -> 25.4 us
  waiting for transfers between devices: 3.89 us -> 11.1 us
  Pallas kernels: 24.5 us -> 18.9 us
  local copies, waits for them, and re-layouts: 4.02 us -> 2.39 us
    all_to_all x4 -> x2, blocking collectives: 73.9 us -> 44.5 us  [exchange(): return lax.all_to_all(pieces, axis, 0, 0, tiled=True)]
    all_to_all x1, starting transfers between devices: 7.89 us -> 22 us  [exchange(): return lax.all_to_all(pieces, axis, 0, 0, tiled=True)]
    all_to_all x1, waiting for transfers between devices: 0.5 us -> 5.17 us  [exchange(): return lax.all_to_all(pieces, axis, 0, 0, tiled=True)]
    pallas_call x3 -> x2, Pallas kernels: 12.7 us -> 9.22 us  [the longest x1 8.28 us: per_device(): call(attend_kernel, (zs * ys, piece, LANES), [SMEM, SMEM, VMEM, VMEM, VMEM])]
    ppermute x1, waiting for transfers between devices: 3.4 us -> 5.9 us  [per_device(): other = lax.ppermute(send, 'xl', [(0, 1), (1, 0)])]
    pallas_call x1, Pallas kernels: 1.78 us -> 0.55 us  [per_device(): partials = call(join_kernel, (phases, piece, LANES), [VMEM])(partials)]
  transfers between devices with their start and end apart: 2 -> 2, of which waited for: 2 -> 2; matrix products, arithmetic and copies ran while one was open for 1% -> 0% of each run, Pallas kernels for 7% -> 8%
where the time goes in v3:
time: 103 us
  blocking collectives  44.5 us (43%)
  starting transfers between devices  25.4 us (25%)
  Pallas kernels  18.9 us (18%)
  waiting for transfers between devices  11.1 us (11%)
  local copies, waits for them, and re-layouts  2.39 us (2%)
    all_to_all x2, blocking collectives, exchange(): return lax.all_to_all(pieces, axis, 0, 0, tiled=True)  44.5 us
    all_to_all x1, starting transfers between devices, exchange(): return lax.all_to_all(pieces, axis, 0, 0, tiled=True)  22 us
    pallas_call x1, Pallas kernels, per_device(): call(attend_kernel, (zs * ys, piece, LANES), [SMEM, SMEM, VMEM, VMEM, VMEM])  8.28 us
    pallas_call x1, Pallas kernels, per_device(): pl.pallas_call(project_kernel, grid=(depth // chunk,), in_specs=[SMEM, pl...  8.23 us
    ppermute x1, waiting for transfers between devices, per_device(): other = lax.ppermute(send, 'xl', [(0, 1), (1, 0)])  5.9 us
    all_to_all x1, waiting for transfers between devices, exchange(): return lax.all_to_all(pieces, axis, 0, 0, tiled=True)  5.17 us
    ppermute x1, starting transfers between devices, per_device(): other = lax.ppermute(send, 'xl', [(0, 1), (1, 0)])  3.39 us
    unnamed x8, local copies, waits for them, and re-layouts  2.39 us
  transfers between devices with their start and end apart: 2, of which 2 were waited for; matrix products, arithmetic and copies ran while one was open for 0% of the time, Pallas kernels for 8%

profile of v3, /device:TPU:16, one launch (start us, length us, event | category | flops | bytes accessed | tf_op | source)
XLA Modules:
  0.0 102.5 jit_solution(8063151964469144361)
XLA Ops:
  0.0 0.0 copy-start.1
  0.0 0.8 copy-done.1
  0.8 0.0 copy-start.2
  0.8 0.7 copy-done.2
  1.4 0.9 shard_map.64
  2.4 22.0 %all-to-all-start = ((bf16[32,80,128]{2,1,0:T(8,128)(2,1)}), bf16[32,80,128]{2,1,0:T(8,128)(2,1)S(1)}, u32[]{:S(2)}, u32[]{:S(2)}) async-start(bf16[32,80,128]{2,1,0:T(8,128)(2,1)} %shard_map.64), calls=%async_computation | async-start | bytes 1310720 | tf_op jit(solution)/shard_map/all_to_all | solution.py:217
  24.4 0.0 copy-start.3
  24.4 8.2 %shard_map.65 = (bf16[2,512,128]{2,1,0:T(8,128)(2,1)}, bf16[2,512,128]{2,1,0:T(8,128)(2,1)}) custom-call(s32[1]{0:T(128)} %bitcast.2.side_ref, bf16[512,4096]{1,0:T(8,128)(2,1)} %x_ref.1, bf16[4096,256]{1,0:T(8,128)(2,1)} %kw_ref.1, bf16[4096,256]{1,0:T(8,128)(2,1)} %vw_ref.1), custom_call_target="tpu_custom_call" | custom-call | flops 2147483648 | bytes 8388608 | tf_op jit(solution)/shard_map/pallas_call | solution.py:224
  32.6 3.4 %collective-permute-start = (bf16[2,512,128]{2,1,0:T(8,128)(2,1)}, bf16[2,512,128]{2,1,0:T(8,128)(2,1)S(1)}, u32[]{:S(2)}, u32[]{:S(2)}) collective-permute-start(bf16[2,512,128]{2,1,0:T(8,128)(2,1)} %get-tuple-element.8), channel_id=1, source_target_pairs={{0,128},{128,0},{1,129},{129,1},{2,130},{130,2},{3,131},{131,3},{4... | collective-permute-start | bytes 786440 | tf_op jit(solution)/shard_map/ppermute | solution.py:244
  36.0 0.1 pad_add_fusion.tiles_ref
  36.1 0.0 copy-done.3
  36.1 0.2 select_reduce_fusion.bits_ref
  36.3 5.9 %collective-permute-done.other_ref = bf16[2,512,128]{2,1,0:T(8,128)(2,1)S(1)} collective-permute-done((bf16[2,512,128]{2,1,0:T(8,128)(2,1)}, bf16[2,512,128]{2,1,0:T(8,128)(2,1)S(1)}, u32[]{:S(2)}, u32[]{:S(2)}) %collective-permute-start) | collective-permute-done | bytes 262176 | tf_op jit(solution)/shard_map/ppermute | solution.py:244
  42.2 5.2 %all-to-all-done.q_ref = bf16[32,80,128]{2,1,0:T(8,128)(2,1)S(1)} async-done(((bf16[32,80,128]{2,1,0:T(8,128)(2,1)}), bf16[32,80,128]{2,1,0:T(8,128)(2,1)S(1)}, u32[]{:S(2)}, u32[]{:S(2)}) %all-to-all-start) | async-done | bytes 655392 | tf_op jit(solution)/shard_map/all_to_all | solution.py:217
  47.4 0.0 copy-start
  47.4 0.9 copy-done
  48.3 8.3 %shard_map.66 = bf16[32,80,128]{2,1,0:T(8,128)(2,1)S(1)} custom-call(s32[2]{0:T(128)S(1)} %pad_add_fusion.tiles_ref, s32[2,32]{1,0:T(2,128)S(1)} %select_reduce_fusion.bits_ref, bf16[32,80,128]{2,1,0:T(8,128)(2,1)S(1)} %all-to-all-done.q_ref, bf16[2,512,128]{2,1,0:T(8,128)(2,1)S(1)} %copy-done, bf16[2,512,128]{2,1,0:T(8,128)(2,1)S(1)} %collective-permute-done.other_ref), custom_call_target="tpu_custom_call" | custom-call | tf_op jit(solution)/shard_map/pallas_call | solution.py:248
  56.6 28.5 %all_to_all.15.in_ref = bf16[32,80,128]{2,1,0:T(8,128)(2,1)S(1)} all-to-all(bf16[32,80,128]{2,1,0:T(8,128)(2,1)S(1)} %shard_map.66), channel_id=1, replica_groups=mesh['xh'=4,'xl'=2,'zh'=4,'y'=8,'head'=4] {'zh','y'}, dimensions={0} | all-to-all | bytes 1310720 | tf_op jit(solution)/shard_map/all_to_all | solution.py:217
  85.1 0.5 shard_map.67
  85.7 16.0 %all_to_all.16.in_ref = bf16[8,80,128]{2,1,0:T(8,128)(2,1)S(1)} all-to-all(bf16[8,80,128]{2,1,0:T(8,128)(2,1)S(1)} %shard_map.67), channel_id=1, replica_groups=mesh['xh'=4,'xl'=2,'zh'=4,'y'=8,'head'=4] {'xh','xl'}, dimensions={0} | all-to-all | bytes 327680 | tf_op jit(solution)/shard_map/all_to_all | solution.py:217
  101.6 0.9 shard_map.68
Async XLA Ops:
  0.0 0.8 copy-start.1
  0.8 0.7 copy-start.2
  2.4 45.0 %all-to-all-start = ((bf16[32,80,128]{2,1,0:T(8,128)(2,1)}), bf16[32,80,128]{2,1,0:T(8,128)(2,1)S(1)}, u32[]{:S(2)}, u32[]{:S(2)}) async-start(bf16[32,80,128]{2,1,0:T(8,128)(2,1)} %shard_map.64), calls=%async_computation | async-start | bytes 1310720 | tf_op jit(solution)/shard_map/all_to_all | solution.py:217
  24.4 11.7 %copy-start.3 = (s32[32,256]{1,0:T(8,128)S(1)}, s32[32,256]{1,0:T(8,128)}, u32[]{:S(2)}) copy-start(s32[32,256]{1,0:T(8,128)} %param.11) | copy-start | bytes 98308
  32.6 9.6 %collective-permute-start = (bf16[2,512,128]{2,1,0:T(8,128)(2,1)}, bf16[2,512,128]{2,1,0:T(8,128)(2,1)S(1)}, u32[]{:S(2)}, u32[]{:S(2)}) collective-permute-start(bf16[2,512,128]{2,1,0:T(8,128)(2,1)} %get-tuple-element.8), channel_id=1, source_target_pairs={{0,128},{128,0},{1,129},{129,1},{2,130},{130,2},{3,131},{131,3},{4... | collective-permute-start | bytes 786440 | tf_op jit(solution)/shard_map/ppermute | solution.py:244
  47.4 1.0 copy-start

commit v4 on v3

--- a/solution.py
+++ b/solution.py
@@ -14,9 +14,11 @@
 RATE = math.log2(math.e) / math.sqrt(HD)
 F32 = jnp.float32
 BF16 = jnp.bfloat16
-TOGETHER = 2
+TOGETHER = 4
 UNROLL = 2
+TAIL = 8
 GRANT = 24 << 20
+WHOLE = 60 << 20
 VMEM = pl.BlockSpec(memory_space=pltpu.VMEM)
 SMEM = pl.BlockSpec(memory_space=pltpu.SMEM)
 
@@ -38,8 +40,8 @@
 
 def stats_block(top, total):
     parts = split3(top) + split3(total)
-    rows = row_ids(16)
-    block = jnp.zeros((16, LANES), F32)
+    rows = row_ids(TAIL)
+    block = jnp.zeros((TAIL, LANES), F32)
     for number, part in enumerate(parts):
         block = jnp.where(rows == number, part, block)
     return block.astype(BF16)
@@ -59,19 +61,15 @@
     blocks = [
         q_ref[:, pl.ds(pl.multiple_of(first + g * HD, HD), HD)] for g in range(width // HD)
     ]
-    bounds = bounds_ref[...].astype(F32)
-    lanes = lane_ids(rows)
-    tail = jnp.zeros((rows, LANES), F32)
-    square = (rows, rows)
-    diagonal = lax.broadcasted_iota(jnp.int32, square, 0) == lax.broadcasted_iota(
-        jnp.int32, square, 1
-    )
+    bounds = bounds_ref[...]
+    bounds = jnp.concatenate([bounds, jnp.zeros((2, LANES - rows), jnp.int32)], axis=1)
+    numbers = row_ids(TAIL)
+    tail = jnp.zeros((TAIL, LANES), F32)
     for side in range(2):
-        row = jnp.broadcast_to(bounds[side:side + 1, :], square)
-        value = jnp.sum(jnp.where(diagonal, row, 0.0), axis=1, keepdims=True).astype(jnp.int32)
+        value = bounds[side:side + 1, :]
         pieces = (value >> 9, (value >> 1) & 255, value & 1)
-        for number, piece in enumerate(pieces):
-            tail = jnp.where(lanes == 3 * side + number, piece.astype(F32), tail)
+        for number, digit in enumerate(pieces):
+            tail = jnp.where(numbers == 3 * side + number, digit.astype(F32), tail)
     blocks.append(tail.astype(BF16))
     packed = jnp.concatenate(blocks, axis=0)
     for copy in range(out_ref.shape[0]):
@@ -102,7 +100,7 @@
 def attend_kernel(tiles_ref, bits_ref, q_ref, own_ref, other_ref, out_ref):
     tiles, piece, _ = q_ref.shape
     text = 16
-    rows = piece - text
+    rows = piece - TAIL
     group = rows // text
     vis = own_ref.shape[1]
     together = TOGETHER
@@ -110,12 +108,12 @@
 
     def step(number, _):
         first = number * together
-        edges = []
+        lines = []
         for at in range(together):
             digits = q_ref[first + at, rows:, :].astype(F32)
-            lower = digits[:, 0:1] * 512 + digits[:, 1:2] * 2 + digits[:, 2:3]
-            upper = digits[:, 3:4] * 512 + digits[:, 4:5] * 2 + digits[:, 5:6]
-            edges.append((lower, upper))
+            lines.append(digits[0:1] * 512 + digits[1:2] * 2 + digits[2:3])
+            lines.append(digits[3:4] * 512 + digits[4:5] * 2 + digits[5:6])
+        edges = jnp.concatenate(lines, axis=0).T[:text]
         queries = jnp.concatenate([q_ref[first + at, :rows, :] for at in range(together)], axis=0)
         scores, tops = [], []
         for source, kv_ref in enumerate((own_ref, other_ref)):
@@ -125,7 +123,7 @@
             ).reshape(together, group, text, vis)
             parts = []
             for at in range(together):
-                lower, upper = edges[at]
+                lower, upper = edges[:, 2 * at:2 * at + 1], edges[:, 2 * at + 1:2 * at + 2]
                 hidden = (1 - bits_ref[source, first + at]).astype(F32) * 1e7
                 visible = (columns >= lower - start + hidden) & (columns < upper - start)
                 bias = jnp.where(visible, 0.0, HIDDEN)
@@ -159,7 +157,7 @@
 
 def joined(pieces):
     n = len(pieces)
-    rows = pieces[0].shape[0] - 16
+    rows = pieces[0].shape[0] - TAIL
     stats = [read_stats(piece[rows:, :]) for piece in pieces]
     tops = jnp.concatenate([top for top, _ in stats], axis=0)
     totals = jnp.concatenate([total for _, total in stats], axis=0)
@@ -192,10 +190,10 @@
             out_ref[:, first:first + HD] = result[g * text:(g + 1) * text]
 
 
-def call(kernel, out, in_specs):
+def call(kernel, out, in_specs, grant=GRANT):
     return pl.pallas_call(
         kernel, out_shape=jax.ShapeDtypeStruct(out, BF16), in_specs=in_specs, out_specs=VMEM,
-        compiler_params=pltpu.CompilerParams(vmem_limit_bytes=GRANT),
+        compiler_params=pltpu.CompilerParams(vmem_limit_bytes=grant),
     )
 
 
@@ -204,7 +202,7 @@
     width = key_weight.shape[1]
     text = queries.shape[0]
     rows = queries.shape[1] // HD // 2 * text
-    piece = rows + text
+    piece = rows + TAIL
     zs, ys = lax.axis_size("zh"), lax.axis_size("y")
     phases = lax.axis_size("xh") * 2
     side = lax.axis_index("xl")
@@ -216,7 +214,9 @@
     def exchange(pieces, axis):
         return lax.all_to_all(pieces, axis, 0, 0, tiled=True)
 
-    packed = call(pack_kernel, (zs * ys, piece, LANES), [SMEM, VMEM, VMEM])(side, queries, bounds.T)
+    packed = call(pack_kernel, (zs * ys, piece, LANES), [SMEM, VMEM, VMEM], WHOLE)(
+        side, queries, bounds.T
+    )
     gathered = exchange(packed, ("zh", "y"))
 
     chunk = 512
@@ -233,7 +233,7 @@
         out_specs=[half, half],
         out_shape=[jax.ShapeDtypeStruct((2, vis_rows, HD), BF16)] * 2,
         scratch_shapes=[pltpu.VMEM((vis_rows, width), F32)] * 2,
-        compiler_params=pltpu.CompilerParams(dimension_semantics=("arbitrary",), vmem_limit_bytes=62 << 20
+        compiler_params=pltpu.CompilerParams(dimension_semantics=("arbitrary",), vmem_limit_bytes=WHOLE
         ),
         cost_estimate=pl.CostEstimate(
             flops=4 * vis_rows * depth * width,

time: 103 us -> 97.9 us (0.950)
  Pallas kernels: 18.9 us -> 16.8 us
  local copies, waits for them, and re-layouts: 2.39 us -> 0.96 us
  waiting for transfers between devices: 11.1 us -> 9.75 us
    pallas_call x1, Pallas kernels: 8.28 us -> 5.51 us  [per_device(): call(attend_kernel, (zs * ys, piece, LANES), [SMEM, SMEM, VMEM, VMEM, VMEM])]
    unnamed x8 -> x4, local copies, waits for them, and re-layouts: 2.39 us -> 0.96 us
    all_to_all x1, waiting for transfers between devices: 5.17 us -> 3.85 us  [exchange(): return lax.all_to_all(pieces, axis, 0, 0, tiled=True)]
where the time goes in v4:
time: 97.9 us; the launch traced here: 97.4 us
  blocking collectives  44.2 us (45%)
  starting transfers between devices  25.4 us (26%)
  Pallas kernels  16.8 us (17%)
  waiting for transfers between devices  9.75 us (10%)
    all_to_all x2, blocking collectives, exchange(): return lax.all_to_all(pieces, axis, 0, 0, tiled=True)  44.2 us
    all_to_all x1, starting transfers between devices, exchange(): return lax.all_to_all(pieces, axis, 0, 0, tiled=True)  22 us
    pallas_call x1, Pallas kernels, per_device(): pl.pallas_call(project_kernel, grid=(depth // chunk,), in_specs=[SMEM, pl...  8.23 us
    ppermute x1, waiting for transfers between devices, per_device(): other = lax.ppermute(send, 'xl', [(0, 1), (1, 0)])  5.9 us
    pallas_call x1, Pallas kernels, per_device(): call(attend_kernel, (zs * ys, piece, LANES), [SMEM, SMEM, VMEM, VMEM, VMEM])  5.51 us
    all_to_all x1, waiting for transfers between devices, exchange(): return lax.all_to_all(pieces, axis, 0, 0, tiled=True)  3.85 us
    ppermute x1, starting transfers between devices, per_device(): other = lax.ppermute(send, 'xl', [(0, 1), (1, 0)])  3.39 us
  transfers between devices with their start and end apart: 2, of which 2 were waited for; matrix products, arithmetic and copies ran while one was open for 0% of the time, Pallas kernels for 8%

profile of v4, /device:TPU:16, one launch (start us, length us, event | category | flops | bytes accessed | tf_op | source)
XLA Modules:
  0.0 97.4 jit_solution(7706737776623318544)
XLA Ops:
  0.0 1.7 %shard_map.64 = bf16[32,72,128]{2,1,0:T(8,128)(2,1)} custom-call(s32[1]{0:T(128)} %bitcast.2.side_ref, bf16[16,1024]{1,0:T(8,128)(2,1)} %q_ref.1, s32[2,16]{1,0:T(2,128)} %bitcast.4), custom_call_target="tpu_custom_call" | custom-call | tf_op jit(solution)/shard_map/pallas_call | solution.py:217
  1.7 22.0 %all-to-all-start = ((bf16[32,72,128]{2,1,0:T(8,128)(2,1)}), bf16[32,72,128]{2,1,0:T(8,128)(2,1)S(1)}, u32[]{:S(2)}, u32[]{:S(2)}) async-start(bf16[32,72,128]{2,1,0:T(8,128)(2,1)} %shard_map.64), calls=%async_computation | async-start | bytes 1179648 | tf_op jit(solution)/shard_map/all_to_all | solution.py:215
  23.6 0.0 copy-start.1
  23.6 8.2 %shard_map.65 = (bf16[2,512,128]{2,1,0:T(8,128)(2,1)}, bf16[2,512,128]{2,1,0:T(8,128)(2,1)}) custom-call(s32[1]{0:T(128)} %bitcast.2.side_ref, bf16[512,4096]{1,0:T(8,128)(2,1)} %x_ref.1, bf16[4096,256]{1,0:T(8,128)(2,1)} %kw_ref.1, bf16[4096,256]{1,0:T(8,128)(2,1)} %vw_ref.1), custom_call_target="tpu_custom_call" | custom-call | flops 2147483648 | bytes 8388608 | tf_op jit(solution)/shard_map/pallas_call | solution.py:224
  31.9 3.4 %collective-permute-start = (bf16[2,512,128]{2,1,0:T(8,128)(2,1)}, bf16[2,512,128]{2,1,0:T(8,128)(2,1)S(1)}, u32[]{:S(2)}, u32[]{:S(2)}) collective-permute-start(bf16[2,512,128]{2,1,0:T(8,128)(2,1)} %get-tuple-element.8), channel_id=1, source_target_pairs={{0,128},{128,0},{1,129},{129,1},{2,130},{130,2},{3,131},{131,3},{4... | collective-permute-start | bytes 786440 | tf_op jit(solution)/shard_map/ppermute | solution.py:244
  35.3 0.1 pad_add_fusion.tiles_ref
  35.4 0.0 copy-done.1
  35.4 0.2 select_reduce_fusion.bits_ref
  35.5 5.9 %collective-permute-done.other_ref = bf16[2,512,128]{2,1,0:T(8,128)(2,1)S(1)} collective-permute-done((bf16[2,512,128]{2,1,0:T(8,128)(2,1)}, bf16[2,512,128]{2,1,0:T(8,128)(2,1)S(1)}, u32[]{:S(2)}, u32[]{:S(2)}) %collective-permute-start) | collective-permute-done | bytes 262176 | tf_op jit(solution)/shard_map/ppermute | solution.py:244
  41.5 3.9 %all-to-all-done.q_ref = bf16[32,72,128]{2,1,0:T(8,128)(2,1)S(1)} async-done(((bf16[32,72,128]{2,1,0:T(8,128)(2,1)}), bf16[32,72,128]{2,1,0:T(8,128)(2,1)S(1)}, u32[]{:S(2)}, u32[]{:S(2)}) %all-to-all-start) | async-done | bytes 589856 | tf_op jit(solution)/shard_map/all_to_all | solution.py:215
  45.3 0.0 copy-start
  45.3 0.9 copy-done
  46.3 5.5 %shard_map.66 = bf16[32,72,128]{2,1,0:T(8,128)(2,1)S(1)} custom-call(s32[2]{0:T(128)S(1)} %pad_add_fusion.tiles_ref, s32[2,32]{1,0:T(2,128)S(1)} %select_reduce_fusion.bits_ref, bf16[32,72,128]{2,1,0:T(8,128)(2,1)S(1)} %all-to-all-done.q_ref, bf16[2,512,128]{2,1,0:T(8,128)(2,1)S(1)} %copy-done, bf16[2,512,128]{2,1,0:T(8,128)(2,1)S(1)} %collective-permute-done.other_ref), custom_call_target="tpu_custom_call" | custom-call | tf_op jit(solution)/shard_map/pallas_call | solution.py:248
  51.8 28.4 %all_to_all.15.in_ref = bf16[32,72,128]{2,1,0:T(8,128)(2,1)S(1)} all-to-all(bf16[32,72,128]{2,1,0:T(8,128)(2,1)S(1)} %shard_map.66), channel_id=1, replica_groups=mesh['xh'=4,'xl'=2,'zh'=4,'y'=8,'head'=4] {'zh','y'}, dimensions={0} | all-to-all | bytes 1179648 | tf_op jit(solution)/shard_map/all_to_all | solution.py:215
  80.1 0.5 shard_map.67
  80.7 15.8 %all_to_all.16.in_ref = bf16[8,72,128]{2,1,0:T(8,128)(2,1)S(1)} all-to-all(bf16[8,72,128]{2,1,0:T(8,128)(2,1)S(1)} %shard_map.67), channel_id=1, replica_groups=mesh['xh'=4,'xl'=2,'zh'=4,'y'=8,'head'=4] {'xh','xl'}, dimensions={0} | all-to-all | bytes 294912 | tf_op jit(solution)/shard_map/all_to_all | solution.py:215
  96.5 0.9 shard_map.68
Async XLA Ops:
  1.7 43.6 %all-to-all-start = ((bf16[32,72,128]{2,1,0:T(8,128)(2,1)}), bf16[32,72,128]{2,1,0:T(8,128)(2,1)S(1)}, u32[]{:S(2)}, u32[]{:S(2)}) async-start(bf16[32,72,128]{2,1,0:T(8,128)(2,1)} %shard_map.64), calls=%async_computation | async-start | bytes 1179648 | tf_op jit(solution)/shard_map/all_to_all | solution.py:215
  23.6 11.7 %copy-start.1 = (s32[32,256]{1,0:T(8,128)S(1)}, s32[32,256]{1,0:T(8,128)}, u32[]{:S(2)}) copy-start(s32[32,256]{1,0:T(8,128)} %param.11) | copy-start | bytes 98308
  31.9 9.6 %collective-permute-start = (bf16[2,512,128]{2,1,0:T(8,128)(2,1)}, bf16[2,512,128]{2,1,0:T(8,128)(2,1)S(1)}, u32[]{:S(2)}, u32[]{:S(2)}) collective-permute-start(bf16[2,512,128]{2,1,0:T(8,128)(2,1)} %get-tuple-element.8), channel_id=1, source_target_pairs={{0,128},{128,0},{1,129},{129,1},{2,130},{130,2},{3,131},{131,3},{4... | collective-permute-start | bytes 786440 | tf_op jit(solution)/shard_map/ppermute | solution.py:244
  45.3 1.0 copy-start

commit v5 on v4

--- a/solution.py
+++ b/solution.py
@@ -19,6 +19,8 @@
 TAIL = 8
 GRANT = 24 << 20
 WHOLE = 60 << 20
+ROOM = 52 << 20
+CHUNK = 512
 VMEM = pl.BlockSpec(memory_space=pltpu.VMEM)
 SMEM = pl.BlockSpec(memory_space=pltpu.SMEM)
 
@@ -76,20 +78,32 @@
         out_ref[copy] = packed
 
 
-def project_kernel(side_ref, x_ref, kw_ref, vw_ref, keep_ref, send_ref, k_acc, v_acc):
-    step = pl.program_id(0)
-
-    @pl.when(step == 0)
-    def _():
-        k_acc[...] = jnp.zeros_like(k_acc)
-        v_acc[...] = jnp.zeros_like(v_acc)
-
-    x = x_ref[...]
-    k_acc[...] += jnp.dot(x, kw_ref[...], preferred_element_type=F32)
-    v_acc[...] += jnp.dot(x, vw_ref[...], preferred_element_type=F32)
-
+def project_kernel(side_ref, x_ref, kw_ref, vw_ref, keep_ref, send_ref, x_buf, kw_buf, vw_buf, k_acc, v_acc, sems):
+    chunks, _, chunk = x_buf.shape
+    copies = []
+    for c in range(chunks):
+        span = slice(c * chunk, (c + 1) * chunk)
+        copies.append((
+            pltpu.make_async_copy(x_ref.at[:, span], x_buf.at[c], sems.at[c, 0]),
+            pltpu.make_async_copy(kw_ref.at[span, :], kw_buf.at[c], sems.at[c, 1]),
+            pltpu.make_async_copy(vw_ref.at[span, :], vw_buf.at[c], sems.at[c, 2]),
+        ))
+    for group in copies:
+        for copy in group:
+            copy.start()
+    for c, group in enumerate(copies):
+        for copy in group:
+            copy.wait()
+        x = x_buf[c]
+        k_part = jnp.dot(x, kw_buf[c], preferred_element_type=F32)
+        v_part = jnp.dot(x, vw_buf[c], preferred_element_type=F32)
+        if c:
+            k_part += k_acc[...]
+            v_part += v_acc[...]
+        k_acc[...] = k_part
+        v_acc[...] = v_part
     for side in range(2):
-        @pl.when((step == pl.num_programs(0) - 1) & (side_ref[0] == side))
+        @pl.when(side_ref[0] == side)
         def _():
             for head, out_ref in ((side, keep_ref), (1 - side, send_ref)):
                 columns = slice(head * HD, (head + 1) * HD)
@@ -197,9 +211,34 @@
     )
 
 
-def per_device(visual, key_weight, value_weight, queries, bounds, tile_mask):
+def project(side, visual, key_weight, value_weight):
     vis_rows, depth = visual.shape
     width = key_weight.shape[1]
+    chunks, chunk = depth // CHUNK, CHUNK
+    anywhere = pl.BlockSpec(memory_space=pl.ANY)
+    return pl.pallas_call(
+        project_kernel,
+        in_specs=[SMEM, anywhere, anywhere, anywhere],
+        out_specs=[VMEM, VMEM],
+        out_shape=[jax.ShapeDtypeStruct((2, vis_rows, HD), BF16)] * 2,
+        scratch_shapes=[
+            pltpu.VMEM((chunks, vis_rows, chunk), BF16),
+            pltpu.VMEM((chunks, chunk, width), BF16),
+            pltpu.VMEM((chunks, chunk, width), BF16),
+            pltpu.VMEM((vis_rows, width), F32),
+            pltpu.VMEM((vis_rows, width), F32),
+            pltpu.SemaphoreType.DMA((chunks, 3)),
+        ],
+        compiler_params=pltpu.CompilerParams(vmem_limit_bytes=ROOM),
+        cost_estimate=pl.CostEstimate(
+            flops=4 * vis_rows * depth * width,
+            bytes_accessed=2 * depth * (vis_rows + 2 * width),
+            transcendentals=0,
+        ),
+    )(side, visual, key_weight, value_weight)
+
+
+def per_device(visual, key_weight, value_weight, queries, bounds, tile_mask):
     text = queries.shape[0]
     rows = queries.shape[1] // HD // 2 * text
     piece = rows + TAIL
@@ -219,28 +258,7 @@
     )
     gathered = exchange(packed, ("zh", "y"))
 
-    chunk = 512
-    half = pl.BlockSpec((2, vis_rows, HD), lambda i: (0, 0, 0))
-    keep, send = pl.pallas_call(
-        project_kernel,
-        grid=(depth // chunk,),
-        in_specs=[
-            SMEM,
-            pl.BlockSpec((vis_rows, chunk), lambda i: (0, i)),
-            pl.BlockSpec((chunk, width), lambda i: (i, 0)),
-            pl.BlockSpec((chunk, width), lambda i: (i, 0)),
-        ],
-        out_specs=[half, half],
-        out_shape=[jax.ShapeDtypeStruct((2, vis_rows, HD), BF16)] * 2,
-        scratch_shapes=[pltpu.VMEM((vis_rows, width), F32)] * 2,
-        compiler_params=pltpu.CompilerParams(dimension_semantics=("arbitrary",), vmem_limit_bytes=WHOLE
-        ),
-        cost_estimate=pl.CostEstimate(
-            flops=4 * vis_rows * depth * width,
-            bytes_accessed=2 * depth * (vis_rows + 2 * width),
-            transcendentals=0,
-        ),
-    )(side, visual, key_weight, value_weight)
+    keep, send = project(side, visual, key_weight, value_weight)
     other = lax.ppermute(send, "xl", [(0, 1), (1, 0)])
 
     tile_ids = lax.broadcasted_iota(jnp.int32, tile_mask.shape, 1)

time: 97.9 us -> 93.6 us (0.956)
  waiting for transfers between devices: 9.75 us -> 13.8 us
  Pallas kernels: 16.8 us -> 12.8 us
  blocking collectives: 44.2 us -> 40.9 us
    all_to_all x1, waiting for transfers between devices: 3.85 us -> 8.08 us  [exchange(): return lax.all_to_all(pieces, axis, 0, 0, tiled=True)]
    pallas_call x1, Pallas kernels: 8.23 us -> 4.19 us  [project(): pl.pallas_call(project_kernel, in_specs=[SMEM, anywhere, anywhere, anywhe...]
    all_to_all x2, blocking collectives: 44.2 us -> 40.9 us  [exchange(): return lax.all_to_all(pieces, axis, 0, 0, tiled=True)]
  transfers between devices with their start and end apart: 2 -> 2, of which waited for: 2 -> 2; matrix products, arithmetic and copies ran while one was open for 0% -> 0% of each run, Pallas kernels for 8% -> 4%
where the time goes in v5:
time: 93.6 us; the launch traced here: 93.2 us
  blocking collectives  40.9 us (44%)
  starting transfers between devices  25.4 us (27%)
  waiting for transfers between devices  13.8 us (15%)
  Pallas kernels  12.8 us (14%)
    all_to_all x2, blocking collectives, exchange(): return lax.all_to_all(pieces, axis, 0, 0, tiled=True)  40.9 us
    all_to_all x1, starting transfers between devices, exchange(): return lax.all_to_all(pieces, axis, 0, 0, tiled=True)  22 us
    all_to_all x1, waiting for transfers between devices, exchange(): return lax.all_to_all(pieces, axis, 0, 0, tiled=True)  8.08 us
    ppermute x1, waiting for transfers between devices, per_device(): other = lax.ppermute(send, 'xl', [(0, 1), (1, 0)])  5.69 us
    pallas_call x1, Pallas kernels, per_device(): call(attend_kernel, (zs * ys, piece, LANES), [SMEM, SMEM, VMEM, VMEM, VMEM])  5.52 us
    pallas_call x1, Pallas kernels, project(): pl.pallas_call(project_kernel, in_specs=[SMEM, anywhere, anywhere, anywhe...  4.19 us
    ppermute x1, starting transfers between devices, per_device(): other = lax.ppermute(send, 'xl', [(0, 1), (1, 0)])  3.41 us
  transfers between devices with their start and end apart: 2, of which 2 were waited for; matrix products, arithmetic and copies ran while one was open for 0% of the time, Pallas kernels for 4%

profile of v5, /device:TPU:16, one launch (start us, length us, event | category | flops | bytes accessed | tf_op | source)
XLA Modules:
  0.0 93.2 jit_solution(16419954980206540301)
XLA Ops:
  0.0 1.6 %shard_map.64 = bf16[32,72,128]{2,1,0:T(8,128)(2,1)} custom-call(s32[1]{0:T(128)} %bitcast.2.side_ref, bf16[16,1024]{1,0:T(8,128)(2,1)} %q_ref.1, s32[2,16]{1,0:T(2,128)} %bitcast.4), custom_call_target="tpu_custom_call" | custom-call | tf_op jit(solution)/shard_map/pallas_call | solution.py:256
  1.7 22.0 %all-to-all-start = ((bf16[32,72,128]{2,1,0:T(8,128)(2,1)}), bf16[32,72,128]{2,1,0:T(8,128)(2,1)S(1)}, u32[]{:S(2)}, u32[]{:S(2)}) async-start(bf16[32,72,128]{2,1,0:T(8,128)(2,1)} %shard_map.64), calls=%async_computation | async-start | bytes 1179648 | tf_op jit(solution)/shard_map/all_to_all | solution.py:254
  23.6 0.0 copy-start
  23.6 4.2 %shard_map.65 = (bf16[2,512,128]{2,1,0:T(8,128)(2,1)S(1)}, bf16[2,512,128]{2,1,0:T(8,128)(2,1)S(1)}) custom-call(s32[1]{0:T(128)} %bitcast.2.side_ref, bf16[512,4096]{1,0:T(8,128)(2,1)} %x_ref.1, bf16[4096,256]{1,0:T(8,128)(2,1)} %kw_ref.1, bf16[4096,256]{1,0:T(8,128)(2,1)} %vw_ref.1), custom_call_target="tpu_custom_call" | custom-call | flops 2147483648 | bytes 8388608 | tf_op jit(solution)/shard_map/pallas_call | solution.py:219
  27.8 3.4 %collective-permute-start = (bf16[2,512,128]{2,1,0:T(8,128)(2,1)S(1)}, bf16[2,512,128]{2,1,0:T(8,128)(2,1)S(1)}, u32[]{:S(2)}, u32[]{:S(2)}) collective-permute-start(bf16[2,512,128]{2,1,0:T(8,128)(2,1)S(1)} %get-tuple-element.8), channel_id=1, source_target_pairs={{0,128},{128,0},{1,129},{129,1},{2,130},{130,2},{3,131},{131,3},{4... | collective-permute-start | bytes 786440 | tf_op jit(solution)/shard_map/ppermute | solution.py:262
  31.3 0.1 pad_add_fusion.tiles_ref
  31.3 0.0 copy-done
  31.3 0.2 select_reduce_fusion.bits_ref
  31.5 5.7 %collective-permute-done.other_ref = bf16[2,512,128]{2,1,0:T(8,128)(2,1)S(1)} collective-permute-done((bf16[2,512,128]{2,1,0:T(8,128)(2,1)S(1)}, bf16[2,512,128]{2,1,0:T(8,128)(2,1)S(1)}, u32[]{:S(2)}, u32[]{:S(2)}) %collective-permute-start) | collective-permute-done | bytes 262176 | tf_op jit(solution)/shard_map/ppermute | solution.py:262
  37.2 8.1 %all-to-all-done.q_ref = bf16[32,72,128]{2,1,0:T(8,128)(2,1)S(1)} async-done(((bf16[32,72,128]{2,1,0:T(8,128)(2,1)}), bf16[32,72,128]{2,1,0:T(8,128)(2,1)S(1)}, u32[]{:S(2)}, u32[]{:S(2)}) %all-to-all-start) | async-done | bytes 589856 | tf_op jit(solution)/shard_map/all_to_all | solution.py:254
  45.3 5.5 %shard_map.66 = bf16[32,72,128]{2,1,0:T(8,128)(2,1)S(1)} custom-call(s32[2]{0:T(128)S(1)} %pad_add_fusion.tiles_ref, s32[2,32]{1,0:T(2,128)S(1)} %select_reduce_fusion.bits_ref, bf16[32,72,128]{2,1,0:T(8,128)(2,1)S(1)} %all-to-all-done.q_ref, bf16[2,512,128]{2,1,0:T(8,128)(2,1)S(1)} %get-tuple-element.7.own_ref, ...), custom_call_target="tpu_custom_call" | custom-call | tf_op jit(solution)/shard_map/pallas_call | solution.py:266
  50.8 25.2 %all_to_all.15.in_ref = bf16[32,72,128]{2,1,0:T(8,128)(2,1)S(1)} all-to-all(bf16[32,72,128]{2,1,0:T(8,128)(2,1)S(1)} %shard_map.66), channel_id=1, replica_groups=mesh['xh'=4,'xl'=2,'zh'=4,'y'=8,'head'=4] {'zh','y'}, dimensions={0} | all-to-all | bytes 1179648 | tf_op jit(solution)/shard_map/all_to_all | solution.py:254
  76.0 0.5 shard_map.67
  76.6 15.8 %all_to_all.16.in_ref = bf16[8,72,128]{2,1,0:T(8,128)(2,1)S(1)} all-to-all(bf16[8,72,128]{2,1,0:T(8,128)(2,1)S(1)} %shard_map.67), channel_id=1, replica_groups=mesh['xh'=4,'xl'=2,'zh'=4,'y'=8,'head'=4] {'xh','xl'}, dimensions={0} | all-to-all | bytes 294912 | tf_op jit(solution)/shard_map/all_to_all | solution.py:254
  92.3 0.9 shard_map.68
Async XLA Ops:
  1.7 43.6 %all-to-all-start = ((bf16[32,72,128]{2,1,0:T(8,128)(2,1)}), bf16[32,72,128]{2,1,0:T(8,128)(2,1)S(1)}, u32[]{:S(2)}, u32[]{:S(2)}) async-start(bf16[32,72,128]{2,1,0:T(8,128)(2,1)} %shard_map.64), calls=%async_computation | async-start | bytes 1179648 | tf_op jit(solution)/shard_map/all_to_all | solution.py:254
  23.6 7.7 %copy-start = (s32[32,256]{1,0:T(8,128)S(1)}, s32[32,256]{1,0:T(8,128)}, u32[]{:S(2)}) copy-start(s32[32,256]{1,0:T(8,128)} %param.11) | copy-start | bytes 98308
  27.8 9.4 %collective-permute-start = (bf16[2,512,128]{2,1,0:T(8,128)(2,1)S(1)}, bf16[2,512,128]{2,1,0:T(8,128)(2,1)S(1)}, u32[]{:S(2)}, u32[]{:S(2)}) collective-permute-start(bf16[2,512,128]{2,1,0:T(8,128)(2,1)S(1)} %get-tuple-element.8), channel_id=1, source_target_pairs={{0,128},{128,0},{1,129},{129,1},{2,130},{130,2},{3,131},{131,3},{4... | collective-permute-start | bytes 786440 | tf_op jit(solution)/shard_map/ppermute | solution.py:262

commit v6 on v5

--- a/solution.py
+++ b/solution.py
@@ -14,9 +14,10 @@
 RATE = math.log2(math.e) / math.sqrt(HD)
 F32 = jnp.float32
 BF16 = jnp.bfloat16
-TOGETHER = 4
-UNROLL = 2
+TOGETHER = 8
+UNROLL = 1
 TAIL = 8
+TEXT_PART = 8
 GRANT = 24 << 20
 WHOLE = 60 << 20
 ROOM = 52 << 20
@@ -60,8 +61,9 @@
     rows = q_ref.shape[0]
     width = q_ref.shape[1] // 2
     first = side_ref[0] * width
-    blocks = [
-        q_ref[:, pl.ds(pl.multiple_of(first + g * HD, HD), HD)] for g in range(width // HD)
+    heads = [
+        q_ref[:, pl.ds(pl.multiple_of(first + g * HD, HD), HD)].astype(F32)
+        for g in range(width // HD)
     ]
     bounds = bounds_ref[...]
     bounds = jnp.concatenate([bounds, jnp.zeros((2, LANES - rows), jnp.int32)], axis=1)
@@ -72,10 +74,14 @@
         pieces = (value >> 9, (value >> 1) & 255, value & 1)
         for number, digit in enumerate(pieces):
             tail = jnp.where(numbers == 3 * side + number, digit.astype(F32), tail)
-    blocks.append(tail.astype(BF16))
-    packed = jnp.concatenate(blocks, axis=0)
+    part = rows // 2
+    packed = []
+    for half in range(2):
+        blocks = [head[half * part:(half + 1) * part] for head in heads]
+        blocks.append(pltpu.roll(tail, LANES - part, 1) if half else tail)
+        packed.append(jnp.concatenate(blocks, axis=0).astype(BF16))
     for copy in range(out_ref.shape[0]):
-        out_ref[copy] = packed
+        out_ref[copy] = packed[copy % 2]
 
 
 def project_kernel(side_ref, x_ref, kw_ref, vw_ref, keep_ref, send_ref, x_buf, kw_buf, vw_buf, k_acc, v_acc, sems):
@@ -111,12 +117,13 @@
                 out_ref[1] = v_acc[:, columns].astype(BF16)
 
 
-def attend_kernel(tiles_ref, bits_ref, q_ref, own_ref, other_ref, out_ref):
+def attend_kernel(tiles_ref, bits_ref, q_ref, *refs):
+    sources, out_ref = refs[:-1], refs[-1]
     tiles, piece, _ = q_ref.shape
-    text = 16
+    text = TEXT_PART
     rows = piece - TAIL
     group = rows // text
-    vis = own_ref.shape[1]
+    vis = sources[0].shape[1]
     together = TOGETHER
     columns = lax.broadcasted_iota(jnp.int32, (text, vis), 1).astype(F32)
 
@@ -130,7 +137,7 @@
         edges = jnp.concatenate(lines, axis=0).T[:text]
         queries = jnp.concatenate([q_ref[first + at, :rows, :] for at in range(together)], axis=0)
         scores, tops = [], []
-        for source, kv_ref in enumerate((own_ref, other_ref)):
+        for source, kv_ref in enumerate(sources):
             start = (tiles_ref[source] * vis).astype(F32)
             found = lax.dot_general(
                 queries, kv_ref[0], (((1,), (1,)), ((), ())), preferred_element_type=F32
@@ -145,25 +152,27 @@
             masked = jnp.stack(parts).reshape(together * rows, vis)
             scores.append(masked)
             tops.append(jnp.max(masked, axis=1, keepdims=True))
-        top = jnp.maximum(jnp.maximum(tops[0], tops[1]), FLOOR)
+        top = jnp.full((together * rows, 1), FLOOR, F32)
+        for one in tops:
+            top = jnp.maximum(top, one)
         total = jnp.zeros((together * rows, 1), F32)
         summed = jnp.zeros((together * rows, HD), F32)
-        for masked, kv_ref in zip(scores, (own_ref, other_ref)):
+        for masked, kv_ref in zip(scores, sources):
             weights = jnp.exp2((masked - top) * RATE)
             total += jnp.sum(weights, axis=1, keepdims=True)
             summed += jnp.dot(weights.astype(BF16), kv_ref[1], preferred_element_type=F32)
         summed = summed.astype(BF16)
         lanes = lane_ids(LANES)
-        for pair in range(together // 2):
-            cut = slice(pair * LANES, (pair + 1) * LANES)
+        per = LANES // rows
+        for block in range(together // per):
+            cut = slice(block * LANES, (block + 1) * LANES)
             both = jnp.where(lanes == 0, top[cut], jnp.where(lanes == 1, total[cut], 0.0)).T
             both = both[0:8]
-            for half in range(2):
-                at = 2 * pair + half
+            for within in range(per):
+                at = per * block + within
                 out_ref[first + at, :rows, :] = summed[at * rows:(at + 1) * rows]
-                if half:
-                    both = pltpu.roll(both, rows, 1)
-                out_ref[first + at, rows:, :] = stats_block(both[0:1], both[1:2])
+                mine = pltpu.roll(both, LANES - rows * within, 1) if within else both
+                out_ref[first + at, rows:, :] = stats_block(mine[0:1], mine[1:2])
         return 0
 
     lax.fori_loop(0, tiles // together, step, 0, unroll=UNROLL)
@@ -186,22 +195,32 @@
 
 
 def join_kernel(in_ref, out_ref):
-    top, total, _, summed = joined([in_ref.at[s] for s in range(in_ref.shape[0])])
-    piece = jnp.concatenate([summed.astype(BF16), stats_block(top, total)], axis=0)
+    n = in_ref.shape[0]
+    first, second = (joined([in_ref.at[s] for s in range(half, n, 2)]) for half in range(2))
+    rows = first[3].shape[0]
+    lanes = lane_ids(1)
+    top, total = (
+        jnp.where(lanes < rows, first[i], pltpu.roll(second[i], rows, 1)) for i in range(2)
+    )
+    piece = jnp.concatenate(
+        [first[3].astype(BF16), second[3].astype(BF16), stats_block(top, total)], axis=0
+    )
     for copy in range(out_ref.shape[0]):
         out_ref[copy] = piece
 
 
 def finish_kernel(in_ref, out_ref):
     sources = in_ref.shape[0]
-    text = out_ref.shape[0]
+    part = TEXT_PART
     for side in range(2):
         _, _, total, summed = joined([in_ref.at[s] for s in range(side, sources, 2)])
-        result = (summed / total).astype(BF16)
-        group = result.shape[0] // text
+        result = summed / total
+        rows = result.shape[0] // 2
+        group = rows // part
         for g in range(group):
             first = (side * group + g) * HD
-            out_ref[:, first:first + HD] = result[g * text:(g + 1) * text]
+            block = [result[h * rows + g * part:h * rows + (g + 1) * part] for h in range(2)]
+            out_ref[:, first:first + HD] = jnp.concatenate(block, axis=0).astype(BF16)
 
 
 def call(kernel, out, in_specs, grant=GRANT):
@@ -240,34 +259,39 @@
 
 def per_device(visual, key_weight, value_weight, queries, bounds, tile_mask):
     text = queries.shape[0]
-    rows = queries.shape[1] // HD // 2 * text
-    piece = rows + TAIL
-    zs, ys = lax.axis_size("zh"), lax.axis_size("y")
+    heads = queries.shape[1] // HD // 2
+    zs, ys = lax.axis_size("zh"), lax.axis_size("yh") * 2
     phases = lax.axis_size("xh") * 2
     side = lax.axis_index("xl")
-    blk = lax.axis_index("zh") * ys + lax.axis_index("y")
+    blk = lax.axis_index("zh") * ys + lax.axis_index("yh") * 2 + lax.axis_index("yl")
     phase = lax.axis_index("xh") * 2 + side
-    tiles = jnp.stack([phase * (zs * ys) + blk, (phase ^ 1) * (zs * ys) + blk])
+    tiles = jnp.stack([p * (zs * ys) + b for b in (blk, blk ^ 1) for p in (phase, phase ^ 1)])
     side = side.reshape(1)
 
     def exchange(pieces, axis):
         return lax.all_to_all(pieces, axis, 0, 0, tiled=True)
 
-    packed = call(pack_kernel, (zs * ys, piece, LANES), [SMEM, VMEM, VMEM], WHOLE)(
+    half = heads * text // 2 + TAIL
+    whole = heads * text + TAIL
+    blocks = ("zh", "yh", "yl")
+    packed = call(pack_kernel, (zs * ys, half, LANES), [SMEM, VMEM, VMEM], WHOLE)(
         side, queries, bounds.T
     )
-    gathered = exchange(packed, ("zh", "y"))
+    gathered = exchange(packed, blocks)
 
     keep, send = project(side, visual, key_weight, value_weight)
-    other = lax.ppermute(send, "xl", [(0, 1), (1, 0)])
+    swap = [(0, 1), (1, 0)]
+    beside = lax.ppermute(send, "xl", swap)
+    across = lax.ppermute(send, ("xl", "yl"), [(0, 3), (1, 2), (2, 1), (3, 0)])
+    above = lax.ppermute(keep, "yl", swap)
 
     tile_ids = lax.broadcasted_iota(jnp.int32, tile_mask.shape, 1)
     bits = jnp.sum(jnp.where(tile_ids[None] == tiles[:, None, None], tile_mask[None], 0), axis=2)
-    partials = call(attend_kernel, (zs * ys, piece, LANES), [SMEM, SMEM, VMEM, VMEM, VMEM])(
-        tiles, bits, gathered, keep, other
-    )
-    partials = exchange(partials, ("zh", "y"))
-    partials = call(join_kernel, (phases, piece, LANES), [VMEM])(partials)
+    partials = call(attend_kernel, (zs * ys, half, LANES), [SMEM, SMEM] + [VMEM] * 5)(
+        tiles, bits, gathered, keep, beside, above, across
+    )
+    partials = exchange(partials, blocks)
+    partials = call(join_kernel, (phases, whole, LANES), [VMEM])(partials)
     partials = exchange(partials, ("xh", "xl"))
     return call(finish_kernel, queries.shape, [VMEM])(partials)
 
@@ -275,9 +299,10 @@
 def solution(mesh):
     phases, blocks, heads = (mesh.shape[name] for name in ("phase", "blk", "head"))
     fine = jax.sharding.Mesh(
-        mesh.devices.reshape(phases // 2, 2, blocks // 8, 8, heads), ("xh", "xl", "zh", "y", "head")
-    )
-    phase, blk = ("xh", "xl"), ("zh", "y")
+        mesh.devices.reshape(phases // 2, 2, blocks // 8, 4, 2, heads),
+        ("xh", "xl", "zh", "yh", "yl", "head"),
+    )
+    phase, blk = ("xh", "xl"), ("zh", "yh", "yl")
     return jax.shard_map(
         per_device,
         mesh=fine,

time: 93.6 us -> 95 us (1.015)
  starting transfers between devices: 25.4 us -> 31.2 us
  waiting for transfers between devices: 13.8 us -> 8.59 us
  blocking collectives: 40.9 us -> 42.4 us
    all_to_all x1, waiting for transfers between devices: 8.08 us -> 0.01 us  [exchange(): return lax.all_to_all(pieces, axis, 0, 0, tiled=True)]
    ppermute x1 -> x3, starting transfers between devices: 3.41 us -> 9.21 us  [the longest x1 4.64 us: per_device(): across = lax.ppermute(send, ('xl', 'yl'), [(0, 3), (1, 2), (2, 1), (3, 0)])]
    ppermute x1 -> x3, waiting for transfers between devices: 5.69 us -> 8.59 us  [the longest x1 6.24 us: per_device(): above = lax.ppermute(keep, 'yl', swap)]
    all_to_all x2, blocking collectives: 40.9 us -> 42.4 us  [exchange(): return lax.all_to_all(pieces, axis, 0, 0, tiled=True)]
  transfers between devices with their start and end apart: 2 -> 4, of which waited for: 2 -> 2; matrix products, arithmetic and copies ran while one was open for 0% -> 0% of each run, Pallas kernels for 4% -> 4%
where the time goes in v6:
time: 95 us; the launch traced here: 94.6 us
  blocking collectives  42.4 us (45%)
  starting transfers between devices  31.2 us (33%)
  Pallas kernels  12 us (13%)
  waiting for transfers between devices  8.59 us (9%)
    all_to_all x2, blocking collectives, exchange(): return lax.all_to_all(pieces, axis, 0, 0, tiled=True)  42.4 us
    all_to_all x1, starting transfers between devices, exchange(): return lax.all_to_all(pieces, axis, 0, 0, tiled=True)  22 us
    ppermute x1, waiting for transfers between devices, per_device(): above = lax.ppermute(keep, 'yl', swap)  6.24 us
    pallas_call x1, Pallas kernels, per_device(): call(attend_kernel, (zs * ys, half, LANES), [SMEM, SMEM] + [VMEM] * 5)  4.99 us
    ppermute x1, starting transfers between devices, per_device(): across = lax.ppermute(send, ('xl', 'yl'), [(0, 3), (1, 2), (2, 1), (3, 0)])  4.64 us
    pallas_call x1, Pallas kernels, project(): pl.pallas_call(project_kernel, in_specs=[SMEM, anywhere, anywhere, anywhe...  4.19 us
    ppermute x1, starting transfers between devices, per_device(): beside = lax.ppermute(send, 'xl', swap)  2.43 us
    ppermute x1, waiting for transfers between devices, per_device(): beside = lax.ppermute(send, 'xl', swap)  2.35 us
  transfers between devices with their start and end apart: 4, of which 2 were waited for; matrix products, arithmetic and copies ran while one was open for 0% of the time, Pallas kernels for 4%

profile of v6, /device:TPU:16, one launch (start us, length us, event | category | flops | bytes accessed | tf_op | source)
XLA Modules:
  0.0 94.6 jit_solution(8175551109126459752)
XLA Ops:
  0.0 1.6 %shard_map.64 = bf16[32,40,128]{2,1,0:T(8,128)(2,1)} custom-call(s32[1]{0:T(128)} %bitcast.4.side_ref, bf16[16,1024]{1,0:T(8,128)(2,1)} %q_ref.1, s32[2,16]{1,0:T(2,128)} %bitcast.6), custom_call_target="tpu_custom_call" | custom-call | tf_op jit(solution)/shard_map/pallas_call | solution.py:277
  1.6 22.0 %all-to-all-start = ((bf16[32,40,128]{2,1,0:T(8,128)(2,1)}), bf16[32,40,128]{2,1,0:T(8,128)(2,1)S(1)}, u32[]{:S(2)}, u32[]{:S(2)}) async-start(bf16[32,40,128]{2,1,0:T(8,128)(2,1)} %shard_map.64), calls=%async_computation | async-start | bytes 655360 | tf_op jit(solution)/shard_map/all_to_all | solution.py:272
  23.5 0.0 copy-start
  23.5 4.2 %shard_map.65 = (bf16[2,512,128]{2,1,0:T(8,128)(2,1)S(1)}, bf16[2,512,128]{2,1,0:T(8,128)(2,1)S(1)}) custom-call(s32[1]{0:T(128)} %bitcast.4.side_ref, bf16[512,4096]{1,0:T(8,128)(2,1)} %x_ref.1, bf16[4096,256]{1,0:T(8,128)(2,1)} %kw_ref.1, bf16[4096,256]{1,0:T(8,128)(2,1)} %vw_ref.1), custom_call_target="tpu_custom_call" | custom-call | flops 2147483648 | bytes 8388608 | tf_op jit(solution)/shard_map/pallas_call | solution.py:238
  27.7 2.1 %collective-permute-start.1 = (bf16[2,512,128]{2,1,0:T(8,128)(2,1)S(1)}, bf16[2,512,128]{2,1,0:T(8,128)(2,1)S(1)}, u32[]{:S(2)}, u32[]{:S(2)}) collective-permute-start(bf16[2,512,128]{2,1,0:T(8,128)(2,1)S(1)} %get-tuple-element.7.refs_0_), channel_id=1, source_target_pairs={{0,4},{4,0},{1,5},{5,1},{2,6},{6,2},{3,7},{7,3},{8,12},{12,8},{9,1... | collective-permute-start | bytes 786440 | tf_op jit(solution)/shard_map/ppermute | solution.py:286
  29.9 4.6 %collective-permute-start.2 = (bf16[2,512,128]{2,1,0:T(8,128)(2,1)S(1)}, bf16[2,512,128]{2,1,0:T(8,128)(2,1)S(1)}, u32[]{:S(2)}, u32[]{:S(2)}) collective-permute-start(bf16[2,512,128]{2,1,0:T(8,128)(2,1)S(1)} %get-tuple-element.8), channel_id=1, source_target_pairs={{0,132},{4,128},{128,4},{132,0},{1,133},{5,129},{129,5},{133,1},{2... | collective-permute-start | bytes 786440 | tf_op jit(solution)/shard_map/ppermute | solution.py:285
  34.5 2.4 %collective-permute-start = (bf16[2,512,128]{2,1,0:T(8,128)(2,1)S(1)}, bf16[2,512,128]{2,1,0:T(8,128)(2,1)S(1)}, u32[]{:S(2)}, u32[]{:S(2)}) collective-permute-start(bf16[2,512,128]{2,1,0:T(8,128)(2,1)S(1)} %get-tuple-element.8), channel_id=1, source_target_pairs={{0,128},{128,0},{1,129},{129,1},{2,130},{130,2},{3,131},{131,3},{4... | collective-permute-start | bytes 786440 | tf_op jit(solution)/shard_map/ppermute | solution.py:284
  37.0 0.1 pad_add_fusion.tiles_ref
  37.1 0.0 copy-done
  37.1 0.2 select_reduce_fusion.bits_ref
  37.3 6.2 %collective-permute-done.1.refs_2_ = bf16[2,512,128]{2,1,0:T(8,128)(2,1)S(1)} collective-permute-done((bf16[2,512,128]{2,1,0:T(8,128)(2,1)S(1)}, bf16[2,512,128]{2,1,0:T(8,128)(2,1)S(1)}, u32[]{:S(2)}, u32[]{:S(2)}) %collective-permute-start.1) | collective-permute-done | bytes 262176 | tf_op jit(solution)/shard_map/ppermute | solution.py:286
  43.5 0.0 collective-permute-done.2.refs_3_
  43.5 2.3 %collective-permute-done.refs_1_ = bf16[2,512,128]{2,1,0:T(8,128)(2,1)S(1)} collective-permute-done((bf16[2,512,128]{2,1,0:T(8,128)(2,1)S(1)}, bf16[2,512,128]{2,1,0:T(8,128)(2,1)S(1)}, u32[]{:S(2)}, u32[]{:S(2)}) %collective-permute-start) | collective-permute-done | bytes 262176 | tf_op jit(solution)/shard_map/ppermute | solution.py:284
  45.9 0.0 all-to-all-done.q_ref
  45.9 5.0 %shard_map.66 = bf16[32,40,128]{2,1,0:T(8,128)(2,1)S(1)} custom-call(s32[4]{0:T(128)S(1)} %pad_add_fusion.tiles_ref, s32[4,32]{1,0:T(4,128)S(1)} %select_reduce_fusion.bits_ref, bf16[32,40,128]{2,1,0:T(8,128)(2,1)S(1)} %all-to-all-done.q_ref, bf16[2,512,128]{2,1,0:T(8,128)(2,1)S(1)} %get-tuple-element.7.refs_0_, ...), custom_call_target="tpu_custom_call" | custom-call | tf_op jit(solution)/shard_map/pallas_call | solution.py:290
  50.9 26.6 %all_to_all.15.in_ref = bf16[32,40,128]{2,1,0:T(8,128)(2,1)S(1)} all-to-all(bf16[32,40,128]{2,1,0:T(8,128)(2,1)S(1)} %shard_map.66), channel_id=1, replica_groups=mesh['xh'=4,'xl'=2,'zh'=4,'yh'=4,'yl'=2,'head'=4] {'zh','yh','yl'}, dimensions={0} | all-to-all | bytes 655360 | tf_op jit(solution)/shard_map/all_to_all | solution.py:272
  77.5 0.4 shard_map.67
  77.9 15.8 %all_to_all.16.in_ref = bf16[8,72,128]{2,1,0:T(8,128)(2,1)S(1)} all-to-all(bf16[8,72,128]{2,1,0:T(8,128)(2,1)S(1)} %shard_map.67), channel_id=1, replica_groups=mesh['xh'=4,'xl'=2,'zh'=4,'yh'=4,'yl'=2,'head'=4] {'xh','xl'}, dimensions={0} | all-to-all | bytes 294912 | tf_op jit(solution)/shard_map/all_to_all | solution.py:272
  93.7 0.9 shard_map.68
Async XLA Ops:
  1.6 44.3 %all-to-all-start = ((bf16[32,40,128]{2,1,0:T(8,128)(2,1)}), bf16[32,40,128]{2,1,0:T(8,128)(2,1)S(1)}, u32[]{:S(2)}, u32[]{:S(2)}) async-start(bf16[32,40,128]{2,1,0:T(8,128)(2,1)} %shard_map.64), calls=%async_computation | async-start | bytes 655360 | tf_op jit(solution)/shard_map/all_to_all | solution.py:272
  23.5 13.5 %copy-start = (s32[32,256]{1,0:T(8,128)S(1)}, s32[32,256]{1,0:T(8,128)}, u32[]{:S(2)}) copy-start(s32[32,256]{1,0:T(8,128)} %param.11) | copy-start | bytes 98308
  27.7 15.8 %collective-permute-start.1 = (bf16[2,512,128]{2,1,0:T(8,128)(2,1)S(1)}, bf16[2,512,128]{2,1,0:T(8,128)(2,1)S(1)}, u32[]{:S(2)}, u32[]{:S(2)}) collective-permute-start(bf16[2,512,128]{2,1,0:T(8,128)(2,1)S(1)} %get-tuple-element.7.refs_0_), channel_id=1, source_target_pairs={{0,4},{4,0},{1,5},{5,1},{2,6},{6,2},{3,7},{7,3},{8,12},{12,8},{9,1... | collective-permute-start | bytes 786440 | tf_op jit(solution)/shard_map/ppermute | solution.py:286
  29.9 13.6 %collective-permute-start.2 = (bf16[2,512,128]{2,1,0:T(8,128)(2,1)S(1)}, bf16[2,512,128]{2,1,0:T(8,128)(2,1)S(1)}, u32[]{:S(2)}, u32[]{:S(2)}) collective-permute-start(bf16[2,512,128]{2,1,0:T(8,128)(2,1)S(1)} %get-tuple-element.8), channel_id=1, source_target_pairs={{0,132},{4,128},{128,4},{132,0},{1,133},{5,129},{129,5},{133,1},{2... | collective-permute-start | bytes 786440 | tf_op jit(solution)/shard_map/ppermute | solution.py:285
  34.5 11.3 %collective-permute-start = (bf16[2,512,128]{2,1,0:T(8,128)(2,1)S(1)}, bf16[2,512,128]{2,1,0:T(8,128)(2,1)S(1)}, u32[]{:S(2)}, u32[]{:S(2)}) collective-permute-start(bf16[2,512,128]{2,1,0:T(8,128)(2,1)S(1)} %get-tuple-element.8), channel_id=1, source_target_pairs={{0,128},{128,0},{1,129},{129,1},{2,130},{130,2},{3,131},{131,3},{4... | collective-permute-start | bytes 786440 | tf_op jit(solution)/shard_map/ppermute | solution.py:284

commit v7 on v5

--- a/solution.py
+++ b/solution.py
@@ -15,7 +15,7 @@
 F32 = jnp.float32
 BF16 = jnp.bfloat16
 TOGETHER = 4
-UNROLL = 2
+UNROLL = 4
 TAIL = 8
 GRANT = 24 << 20
 WHOLE = 60 << 20
@@ -56,7 +56,7 @@
     return top, total
 
 
-def pack_kernel(side_ref, q_ref, bounds_ref, out_ref):
+def pack_kernel(side_ref, q_ref, bounds_ref, out_ref, packed, sems):
     rows = q_ref.shape[0]
     width = q_ref.shape[1] // 2
     first = side_ref[0] * width
@@ -73,9 +73,15 @@
         for number, digit in enumerate(pieces):
             tail = jnp.where(numbers == 3 * side + number, digit.astype(F32), tail)
     blocks.append(tail.astype(BF16))
-    packed = jnp.concatenate(blocks, axis=0)
-    for copy in range(out_ref.shape[0]):
-        out_ref[copy] = packed
+    packed[...] = jnp.concatenate(blocks, axis=0)
+    copies = [
+        pltpu.make_async_copy(packed, out_ref.at[copy], sems.at[copy])
+        for copy in range(out_ref.shape[0])
+    ]
+    for copy in copies:
+        copy.start()
+    for copy in copies:
+        copy.wait()
 
 
 def project_kernel(side_ref, x_ref, kw_ref, vw_ref, keep_ref, send_ref, x_buf, kw_buf, vw_buf, k_acc, v_acc, sems):
@@ -253,9 +259,14 @@
     def exchange(pieces, axis):
         return lax.all_to_all(pieces, axis, 0, 0, tiled=True)
 
-    packed = call(pack_kernel, (zs * ys, piece, LANES), [SMEM, VMEM, VMEM], WHOLE)(
-        side, queries, bounds.T
-    )
+    packed = pl.pallas_call(
+        pack_kernel,
+        out_shape=jax.ShapeDtypeStruct((zs * ys, piece, LANES), BF16),
+        in_specs=[SMEM, VMEM, VMEM],
+        out_specs=pl.BlockSpec(memory_space=pl.ANY),
+        scratch_shapes=[pltpu.VMEM((piece, LANES), BF16), pltpu.SemaphoreType.DMA((zs * ys,))],
+        compiler_params=pltpu.CompilerParams(vmem_limit_bytes=WHOLE),
+    )(side, queries, bounds.T)
     gathered = exchange(packed, ("zh", "y"))
 
     keep, send = project(side, visual, key_weight, value_weight)

time: 93.6 us -> 93.5 us (level)
  no operation moved by 1% of the time
where the time goes in v7:
time: 93.5 us; the launch traced here: 93.2 us
  blocking collectives  40.9 us (44%)
  starting transfers between devices  25.4 us (27%)
  waiting for transfers between devices  13.8 us (15%)
  Pallas kernels  12.8 us (14%)
    all_to_all x2, blocking collectives, exchange(): return lax.all_to_all(pieces, axis, 0, 0, tiled=True)  40.9 us
    all_to_all x1, starting transfers between devices, exchange(): return lax.all_to_all(pieces, axis, 0, 0, tiled=True)  22 us
    all_to_all x1, waiting for transfers between devices, exchange(): return lax.all_to_all(pieces, axis, 0, 0, tiled=True)  8.08 us
    ppermute x1, waiting for transfers between devices, per_device(): other = lax.ppermute(send, 'xl', [(0, 1), (1, 0)])  5.69 us
    pallas_call x1, Pallas kernels, per_device(): call(attend_kernel, (zs * ys, piece, LANES), [SMEM, SMEM, VMEM, VMEM, VMEM])  5.26 us
    pallas_call x1, Pallas kernels, project(): pl.pallas_call(project_kernel, in_specs=[SMEM, anywhere, anywhere, anywhe...  4.19 us
    ppermute x1, starting transfers between devices, per_device(): other = lax.ppermute(send, 'xl', [(0, 1), (1, 0)])  3.41 us
  transfers between devices with their start and end apart: 2, of which 2 were waited for; matrix products, arithmetic and copies ran while one was open for 0% of the time, Pallas kernels for 4%

profile of v7, /device:TPU:16, one launch (start us, length us, event | category | flops | bytes accessed | tf_op | source)
XLA Modules:
  0.0 93.2 jit_solution(4620282343485050036)
XLA Ops:
  0.0 1.9 %shard_map.64 = bf16[32,72,128]{2,1,0:T(8,128)(2,1)} custom-call(s32[1]{0:T(128)} %bitcast.2.side_ref, bf16[16,1024]{1,0:T(8,128)(2,1)} %q_ref.1, s32[2,16]{1,0:T(2,128)} %bitcast.4), custom_call_target="tpu_custom_call" | custom-call | tf_op jit(solution)/shard_map/pallas_call | solution.py:262
  1.9 22.0 %all-to-all-start = ((bf16[32,72,128]{2,1,0:T(8,128)(2,1)}), bf16[32,72,128]{2,1,0:T(8,128)(2,1)S(1)}, u32[]{:S(2)}, u32[]{:S(2)}) async-start(bf16[32,72,128]{2,1,0:T(8,128)(2,1)} %shard_map.64), calls=%async_computation | async-start | bytes 1179648 | tf_op jit(solution)/shard_map/all_to_all | solution.py:260
  23.9 0.0 copy-start
  23.9 4.2 %shard_map.65 = (bf16[2,512,128]{2,1,0:T(8,128)(2,1)S(1)}, bf16[2,512,128]{2,1,0:T(8,128)(2,1)S(1)}) custom-call(s32[1]{0:T(128)} %bitcast.2.side_ref, bf16[512,4096]{1,0:T(8,128)(2,1)} %x_ref.1, bf16[4096,256]{1,0:T(8,128)(2,1)} %kw_ref.1, bf16[4096,256]{1,0:T(8,128)(2,1)} %vw_ref.1), custom_call_target="tpu_custom_call" | custom-call | flops 2147483648 | bytes 8388608 | tf_op jit(solution)/shard_map/pallas_call | solution.py:225
  28.1 3.4 %collective-permute-start = (bf16[2,512,128]{2,1,0:T(8,128)(2,1)S(1)}, bf16[2,512,128]{2,1,0:T(8,128)(2,1)S(1)}, u32[]{:S(2)}, u32[]{:S(2)}) collective-permute-start(bf16[2,512,128]{2,1,0:T(8,128)(2,1)S(1)} %get-tuple-element.8), channel_id=1, source_target_pairs={{0,128},{128,0},{1,129},{129,1},{2,130},{130,2},{3,131},{131,3},{4... | collective-permute-start | bytes 786440 | tf_op jit(solution)/shard_map/ppermute | solution.py:273
  31.5 0.1 pad_add_fusion.tiles_ref
  31.6 0.0 copy-done
  31.6 0.2 select_reduce_fusion.bits_ref
  31.8 5.7 %collective-permute-done.other_ref = bf16[2,512,128]{2,1,0:T(8,128)(2,1)S(1)} collective-permute-done((bf16[2,512,128]{2,1,0:T(8,128)(2,1)S(1)}, bf16[2,512,128]{2,1,0:T(8,128)(2,1)S(1)}, u32[]{:S(2)}, u32[]{:S(2)}) %collective-permute-start) | collective-permute-done | bytes 262176 | tf_op jit(solution)/shard_map/ppermute | solution.py:273
  37.5 8.1 %all-to-all-done.q_ref = bf16[32,72,128]{2,1,0:T(8,128)(2,1)S(1)} async-done(((bf16[32,72,128]{2,1,0:T(8,128)(2,1)}), bf16[32,72,128]{2,1,0:T(8,128)(2,1)S(1)}, u32[]{:S(2)}, u32[]{:S(2)}) %all-to-all-start) | async-done | bytes 589856 | tf_op jit(solution)/shard_map/all_to_all | solution.py:260
  45.5 5.3 %shard_map.66 = bf16[32,72,128]{2,1,0:T(8,128)(2,1)S(1)} custom-call(s32[2]{0:T(128)S(1)} %pad_add_fusion.tiles_ref, s32[2,32]{1,0:T(2,128)S(1)} %select_reduce_fusion.bits_ref, bf16[32,72,128]{2,1,0:T(8,128)(2,1)S(1)} %all-to-all-done.q_ref, bf16[2,512,128]{2,1,0:T(8,128)(2,1)S(1)} %get-tuple-element.7.own_ref, ...), custom_call_target="tpu_custom_call" | custom-call | tf_op jit(solution)/shard_map/pallas_call | solution.py:277
  50.8 25.1 %all_to_all.15.in_ref = bf16[32,72,128]{2,1,0:T(8,128)(2,1)S(1)} all-to-all(bf16[32,72,128]{2,1,0:T(8,128)(2,1)S(1)} %shard_map.66), channel_id=1, replica_groups=mesh['xh'=4,'xl'=2,'zh'=4,'y'=8,'head'=4] {'zh','y'}, dimensions={0} | all-to-all | bytes 1179648 | tf_op jit(solution)/shard_map/all_to_all | solution.py:260
  75.9 0.5 shard_map.67
  76.5 15.8 %all_to_all.16.in_ref = bf16[8,72,128]{2,1,0:T(8,128)(2,1)S(1)} all-to-all(bf16[8,72,128]{2,1,0:T(8,128)(2,1)S(1)} %shard_map.67), channel_id=1, replica_groups=mesh['xh'=4,'xl'=2,'zh'=4,'y'=8,'head'=4] {'xh','xl'}, dimensions={0} | all-to-all | bytes 294912 | tf_op jit(solution)/shard_map/all_to_all | solution.py:260
  92.3 0.9 shard_map.68
Async XLA Ops:
  1.9 43.7 %all-to-all-start = ((bf16[32,72,128]{2,1,0:T(8,128)(2,1)}), bf16[32,72,128]{2,1,0:T(8,128)(2,1)S(1)}, u32[]{:S(2)}, u32[]{:S(2)}) async-start(bf16[32,72,128]{2,1,0:T(8,128)(2,1)} %shard_map.64), calls=%async_computation | async-start | bytes 1179648 | tf_op jit(solution)/shard_map/all_to_all | solution.py:260
  23.9 7.7 %copy-start = (s32[32,256]{1,0:T(8,128)S(1)}, s32[32,256]{1,0:T(8,128)}, u32[]{:S(2)}) copy-start(s32[32,256]{1,0:T(8,128)} %param.11) | copy-start | bytes 98308
  28.1 9.4 %collective-permute-start = (bf16[2,512,128]{2,1,0:T(8,128)(2,1)S(1)}, bf16[2,512,128]{2,1,0:T(8,128)(2,1)S(1)}, u32[]{:S(2)}, u32[]{:S(2)}) collective-permute-start(bf16[2,512,128]{2,1,0:T(8,128)(2,1)S(1)} %get-tuple-element.8), channel_id=1, source_target_pairs={{0,128},{128,0},{1,129},{129,1},{2,130},{130,2},{3,131},{131,3},{4... | collective-permute-start | bytes 786440 | tf_op jit(solution)/shard_map/ppermute | solution.py:273
